TPU v7x, 32 devices: a whole 2x2x4 slice. The times are simulated.
32 devices in a mesh: dp: 2 (over x), expert: 16 (over z, y, core).
Axes of the slice: x: 2, y: 2, z: 4, core: 2. Of those that a mesh axis runs over, the one named last changes fastest.
Arguments:
- tokens: bfloat16 [512, 2048], P('expert', 'dp'), may hold values from -6 to 6
- cotangent: bfloat16 [512, 2048], P('expert', 'dp'), may hold values from -6 to 6
- routes: int32 [512, 8], P('expert'), may hold values from 0 to 15, all different within a row; in each aligned block of 32 rows (0 to 31, 32 to 63, ...) at most 20 rows name the same one
- probs: float32 [512, 8], P('expert'), may hold values from 0.03 to 0.6
- matching: int32 [16], replicated, may hold values from 0 to 15, as said below
- gate_weight: bfloat16 [16, 2048, 1024], P('expert', None, 'dp'), may hold values from -0.125 to 0.125
- up_weight: bfloat16 [16, 2048, 1024], P('expert', None, 'dp'), may hold values from -0.125 to 0.125
- down_weight: bfloat16 [16, 2048, 1024], P('expert', None, 'dp'), may hold values from -0.1875 to 0.1875
Outputs:
- input_grad: bfloat16 [512, 2048], P('expert', 'dp')
- gate_weight_grad: float32 [16, 2048, 1024], P('expert', None, 'dp')
- up_weight_grad: float32 [16, 2048, 1024], P('expert', None, 'dp')
- down_weight_grad: float32 [16, 2048, 1024], P('expert', None, 'dp')
Inputs may be any that keep to these rules, and one draw needn't show every extreme that they name: matching pairs the experts: matching[matching[i]] == i and matching[i] != i. `routes`: each token names 8 different experts; within each aligned block of 32 tokens no expert is named by more than 20 tokens.
All inputs are finite; a program needn't handle non-finite values.
Results may differ from a plain program's by a relative error of at most 0.015.
Values may be sent and summed in bfloat16 or wider, within the bound.
A program may use at most 64 MiB of HBM per device.

v0:
```python
import jax
import jax.numpy as jnp
from jax import lax
from jax.sharding import PartitionSpec as P

contract_rows = (((0,), (0,)), ((), ()))
contract_cols = (((1,), (1,)), ((), ()))


def relay_weights(first, second, third):
    return (
        lax.all_to_all(first, "expert", split_axis=1, concat_axis=0, tiled=True),
        lax.all_to_all(second, "expert", split_axis=1, concat_axis=0, tiled=True),
        lax.all_to_all(third, "expert", split_axis=1, concat_axis=0, tiled=True),
    )


def migrate(arrays, matching, mover):
    experts = matching.shape[0]
    model_width = arrays[0].shape[-2]
    hidden_width = arrays[0].shape[-1]
    piece_rows = model_width // experts
    split = [a.reshape(1, experts, piece_rows, hidden_width) for a in arrays]
    spread = mover(split[0], split[1], split[2])
    ordered = [
        jnp.take(s, matching, axis=0).reshape(1, experts, piece_rows, hidden_width) for s in spread
    ]
    landed = mover(ordered[0], ordered[1], ordered[2])
    return [w.reshape(model_width, hidden_width) for w in landed]


def layout(routes, probs, target_table, capacity):
    experts = target_table.shape[0]
    tok_rows = routes.shape[0]
    top_count = routes.shape[1]
    pair_count = tok_rows * top_count
    pair_expert = routes.reshape(pair_count)
    onehot = (pair_expert[:, None] == jnp.arange(experts, dtype=jnp.int32)[None, :]).astype(
        jnp.int32
    )
    running = jnp.cumsum(onehot, axis=0)
    rank = jnp.sum(onehot * running, axis=1) - 1
    target = jnp.sum(onehot * target_table[None, :], axis=1)
    slot = target * capacity + rank
    slot_total = experts * capacity
    owners = jnp.arange(pair_count, dtype=jnp.int32) // top_count
    slot_token = jnp.full((slot_total,), tok_rows, jnp.int32).at[slot].set(owners)
    slot_prob = jnp.zeros((slot_total,), jnp.float32).at[slot].set(probs.reshape(pair_count))
    return (slot, slot_token, slot_prob)


def build_rows(tokens, cotangent, slot_token, slot_prob):
    blank = jnp.zeros((1, tokens.shape[1]), jnp.bfloat16)
    inputs = jnp.take(jnp.concatenate([tokens, blank], axis=0), slot_token, axis=0)
    picked = jnp.take(jnp.concatenate([cotangent, blank], axis=0), slot_token, axis=0)
    grads = (picked.astype(jnp.float32) * slot_prob[:, None]).astype(jnp.bfloat16)
    return (inputs, grads)


def combine_pairs(returned, slot, tok_rows, top_count):
    rows = jnp.take(returned, slot, axis=0)
    return jnp.sum(rows.reshape(tok_rows, top_count, returned.shape[1]), axis=1)


def expert_grads(inputs, grads, w_gate, w_up, w_down):
    gate = jnp.dot(inputs, w_gate, preferred_element_type=jnp.float32)
    upper = jnp.dot(inputs, w_up, preferred_element_type=jnp.float32)
    sig = jax.nn.sigmoid(gate)
    hidden = (gate * sig * upper).astype(jnp.bfloat16)
    hidden_back = jnp.dot(grads, w_down, preferred_element_type=jnp.float32)
    up_back = (hidden_back * gate * sig).astype(jnp.bfloat16)
    gate_back = (hidden_back * upper * sig * (1.0 + gate * (1.0 - sig))).astype(jnp.bfloat16)
    gate_sum = lax.dot_general(inputs, gate_back, contract_rows, preferred_element_type=jnp.float32)
    up_sum = lax.dot_general(inputs, up_back, contract_rows, preferred_element_type=jnp.float32)
    down_sum = lax.dot_general(grads, hidden, contract_rows, preferred_element_type=jnp.float32)
    return (gate_sum, up_sum, down_sum, gate_back, up_back)


def slice_back(gate_back, up_back, w_gate, w_up):
    first = lax.dot_general(gate_back, w_gate, contract_cols, preferred_element_type=jnp.float32)
    return first + lax.dot_general(up_back, w_up, contract_cols, preferred_element_type=jnp.float32)


def local(tokens, cotangent, routes, probs, matching, gate_weight, up_weight, down_weight):
    experts = matching.shape[0]
    tok_rows = routes.shape[0]
    top_count = routes.shape[1]
    capacity = max(2, 5 * tok_rows * top_count // (4 * experts))
    model_width = gate_weight.shape[1]
    hidden_width = gate_weight.shape[2]
    w_gate, w_up, w_down = migrate((gate_weight, up_weight, down_weight), matching, relay_weights)
    slot, slot_token, slot_prob = layout(routes, probs, matching, capacity)
    inputs, grads = build_rows(tokens, cotangent, slot_token, slot_prob)
    part_in, part_out = (
        lax.all_to_all(inputs, "expert", split_axis=0, concat_axis=0, tiled=True),
        lax.all_to_all(grads, "expert", split_axis=0, concat_axis=0, tiled=True),
    )
    arrived_in, arrived_out = (
        lax.all_gather(part_in, "dp", axis=1, tiled=True),
        lax.all_gather(part_out, "dp", axis=1, tiled=True),
    )
    gate_sum, up_sum, down_sum, gate_back, up_back = expert_grads(
        arrived_in, arrived_out, w_gate, w_up, w_down
    )
    partial_value = slice_back(gate_back, up_back, w_gate, w_up).astype(jnp.bfloat16)
    pair_back = lax.psum_scatter(partial_value, "dp", scatter_dimension=1, tiled=True).astype(
        jnp.float32
    )
    returned = lax.all_to_all(
        pair_back.astype(jnp.bfloat16), "expert", split_axis=0, concat_axis=0, tiled=True
    ).astype(pair_back.dtype)
    token_sum = combine_pairs(returned, slot, tok_rows, top_count)
    return (
        token_sum.astype(jnp.bfloat16),
        gate_sum.reshape(1, model_width, hidden_width),
        up_sum.reshape(1, model_width, hidden_width),
        down_sum.reshape(1, model_width, hidden_width),
    )


def solution(mesh):
    placed = (
        P("expert", "dp"),
        P("expert", "dp"),
        P("expert", None),
        P("expert", None),
        P(),
        P("expert", None, "dp"),
        P("expert", None, "dp"),
        P("expert", None, "dp"),
    )
    return jax.shard_map(
        local,
        mesh=mesh,
        in_specs=placed,
        out_specs=(
            P("expert", "dp"),
            P("expert", None, "dp"),
            P("expert", None, "dp"),
            P("expert", None, "dp"),
        ),
        check_vma=False,
    )
```

profile of v0, /device:TPU:0, one launch (start us, length us, event | category | flops | bytes accessed | tf_op | source)
XLA Modules:
  0.0 454.0 jit_solution(13561294605070350274)
XLA Ops:
  16.7 27.3 %all_to_all.96 = bf16[16,20,1024]{2,1,0:T(8,128)(2,1)S(1)} all-to-all(bf16[16,20,1024]{2,1,0:T(8,128)(2,1)S(1)} %all_to_all.70), channel_id=1, replica_groups=mesh['dp'=2,'expert'=16] {'expert'}, dimensions={0} | all-to-all | bytes 1310720 | tf_op jit(solution)/shard_map/all_to_all | solution.py:96
  44.1 51.7 %all_to_all.97 = bf16[1,16,128,512]{3,2,0,1:T(8,128)(2,1)} all-to-all(bf16[1,16,128,512]{3,2,0,1:T(8,128)(2,1)} %bitcast.87), channel_id=1, replica_groups=mesh['dp'=2,'expert'=16] {'expert'}, dimensions={1} | all-to-all | bytes 4194304 | tf_op jit(solution)/shard_map/all_to_all | solution.py:12
  95.8 52.1 %all_to_all.98 = bf16[1,16,128,512]{3,2,0,1:T(8,128)(2,1)} all-to-all(bf16[1,16,128,512]{3,2,0,1:T(8,128)(2,1)S(1)} %bitcast.88), channel_id=1, replica_groups=mesh['dp'=2,'expert'=16] {'expert'}, dimensions={1} | all-to-all | bytes 4194304 | tf_op jit(solution)/shard_map/all_to_all | solution.py:13
  147.9 5.3 %all-to-all-start.1 = ((bf16[1,16,128,512]{3,2,0,1:T(8,128)(2,1)}), bf16[1,16,128,512]{3,2,0,1:T(8,128)(2,1)S(1)}, u32[]{:S(2)}, u32[]{:S(2)}) async-start(bf16[1,16,128,512]{3,2,0,1:T(8,128)(2,1)} %bitcast.89), calls=%async_computation.1 | async-start | bytes 4194304 | tf_op jit(solution)/shard_map/all_to_all | solution.py:14
  153.2 2.6 gather_fusion.3
  160.0 34.2 %all-to-all-done.1 = bf16[1,16,128,512]{3,2,0,1:T(8,128)(2,1)S(1)} async-done(((bf16[1,16,128,512]{3,2,0,1:T(8,128)(2,1)}), bf16[1,16,128,512]{3,2,0,1:T(8,128)(2,1)S(1)}, u32[]{:S(2)}, u32[]{:S(2)}) %all-to-all-start.1) | async-done | bytes 2097184 | tf_op jit(solution)/shard_map/all_to_all | solution.py:14
  194.2 11.3 %all-to-all-start.3 = ((bf16[16,20,1024]{2,1,0:T(8,128)(2,1)}), bf16[16,20,1024]{2,1,0:T(8,128)(2,1)}, u32[]{:S(2)}, u32[]{:S(2)}) async-start(bf16[16,20,1024]{2,1,0:T(8,128)(2,1)} %all_to_all.76), calls=%async_computation.3 | async-start | bytes 1572864 | tf_op jit(solution)/shard_map/all_to_all | solution.py:95
  207.8 3.6 gather_fusion.4
  211.4 3.6 gather_fusion.2
  215.0 5.2 %fusion.2 = (bf16[1,16,128,512]{3,2,0,1:T(8,128)(2,1)}, bf16[1,16,128,512]{3,2,0,1:T(8,128)(2,1)}, bf16[1,16,128,512]{3,2,0,1:T(8,128)(2,1)}) fusion(bf16[16,128,512]{2,1,0:T(8,128)(2,1)} %gather_fusion.4, pred[16]{0:T(512)(128)(4,1)S(1)} %compare_and_fusion.1, bf16[16,128,512]{2,1,0:T(8,128)(2,1)S(1)} %gather_fusion.5, bf16[16,128,512]{2,1,0:T(8,128)(2,1)} %gather_fusion.2), kind=kLoop, calls=%fused_computation.16 | loop fusion | flops 3145728 | bytes 12582928 | tf_op jit(solution)/shard_map/reshape | solution.py:26
  220.1 4.0 all-to-all-done.3
  224.2 52.7 %all_to_all.99 = bf16[1,16,128,512]{3,2,0,1:T(8,128)(2,1)S(1)} all-to-all(bf16[1,16,128,512]{3,2,0,1:T(8,128)(2,1)} %get-tuple-element.10), channel_id=1, replica_groups=mesh['dp'=2,'expert'=16] {'expert'}, dimensions={1} | all-to-all | bytes 4194304 | tf_op jit(solution)/shard_map/all_to_all | solution.py:13
  276.8 52.2 %all_to_all.100 = bf16[1,16,128,512]{3,2,0,1:T(8,128)(2,1)} all-to-all(bf16[1,16,128,512]{3,2,0,1:T(8,128)(2,1)S(1)} %copy-done.1), channel_id=1, replica_groups=mesh['dp'=2,'expert'=16] {'expert'}, dimensions={1} | all-to-all | bytes 4194304 | tf_op jit(solution)/shard_map/all_to_all | solution.py:12
  329.0 5.2 %all-to-all-start.2 = ((bf16[1,16,128,512]{3,2,0,1:T(8,128)(2,1)}), bf16[1,16,128,512]{3,2,0,1:T(8,128)(2,1)}, u32[]{:S(2)}, u32[]{:S(2)}) async-start(bf16[1,16,128,512]{3,2,0,1:T(8,128)(2,1)} %get-tuple-element.12), calls=%async_computation.2 | async-start | bytes 4194304 | tf_op jit(solution)/shard_map/all_to_all | solution.py:14
  337.4 25.3 %all-gather.5.cloned.1.call-done = bf16[320,2048]{1,0:T(8,128)(2,1)} async-done(((bf16[320,1024]{1,0:T(8,128)(2,1)}), bf16[320,2048]{1,0:T(8,128)(2,1)}) %all-gather.5.cloned.1.call-update) | async-done | bytes 1310736 | tf_op jit(solution)/shard_map/all_gather | solution.py:99
  362.7 3.8 fusion.15
  368.1 20.9 %all-gather.3.cloned.1.call-done = bf16[320,2048]{1,0:T(8,128)(2,1)} async-done(((bf16[320,1024]{1,0:T(8,128)(2,1)}), bf16[320,2048]{1,0:T(8,128)(2,1)}) %all-gather.3.cloned.1.call-update) | async-done | bytes 1310736 | tf_op jit(solution)/shard_map/all_gather | solution.py:100
  389.1 3.5 multiply_convert_fusion.2
  395.5 23.4 %reduce-scatter.2.cloned.1.call-done = bf16[320,1024]{1,0:T(8,128)(2,1)} async-done(((bf16[320,2048]{1,0:T(8,128)(2,1)}), bf16[320,1024]{1,0:T(8,128)(2,1)}) %reduce-scatter.2.cloned.1.call-update) | async-done | bytes 655376 | tf_op jit(solution)/shard_map/reduce_scatter | solution.py:106
  420.9 5.6 %all-to-all-start.8 = ((bf16[16,20,1024]{2,1,0:T(8,128)(2,1)}), bf16[16,20,1024]{2,1,0:T(8,128)(2,1)S(1)}, u32[]{:S(2)}, u32[]{:S(2)}) async-start(bf16[16,20,1024]{2,1,0:T(8,128)(2,1)} %all_to_all.85), calls=%async_computation.9 | async-start | bytes 1572864 | tf_op jit(solution)/shard_map/all_to_all | solution.py:109
  426.7 3.3 convolution_bitcast_fusion.1
  430.0 3.3 convolution_bitcast_fusion.2
  433.3 3.4 convolution_bitcast_fusion
  436.7 8.5 %all-to-all-done.8 = bf16[16,20,1024]{2,1,0:T(8,128)(2,1)S(1)} async-done(((bf16[16,20,1024]{2,1,0:T(8,128)(2,1)}), bf16[16,20,1024]{2,1,0:T(8,128)(2,1)S(1)}, u32[]{:S(2)}, u32[]{:S(2)}) %all-to-all-start.8) | async-done | bytes 655392 | tf_op jit(solution)/shard_map/all_to_all | solution.py:109
  (77 shorter events, 28.0 us)
Async XLA Ops:
  44.1 51.7 %copy-start.6 = (bf16[1,2048,512]{2,1,0:T(8,128)(2,1)S(1)}, bf16[1,2048,512]{2,1,0:T(8,128)(2,1)}, u32[]{:S(2)}) copy-start(bf16[1,2048,512]{2,1,0:T(8,128)(2,1)} %param.18) | copy-start | bytes 6291460
  147.9 5.3 %copy-start.9 = (bf16[32,1024]{1,0:T(8,128)(2,1)S(1)}, bf16[32,1024]{1,0:T(8,128)(2,1)}, u32[]{:S(2)}) copy-start(bf16[32,1024]{1,0:T(8,128)(2,1)} %param.12) | copy-start | bytes 196612
  147.9 46.3 %all-to-all-start.1 = ((bf16[1,16,128,512]{3,2,0,1:T(8,128)(2,1)}), bf16[1,16,128,512]{3,2,0,1:T(8,128)(2,1)S(1)}, u32[]{:S(2)}, u32[]{:S(2)}) async-start(bf16[1,16,128,512]{3,2,0,1:T(8,128)(2,1)} %bitcast.89), calls=%async_computation.1 | async-start | bytes 4194304 | tf_op jit(solution)/shard_map/all_to_all | solution.py:14
  155.9 49.6 %copy-start.10 = (s32[16]{0:T(128)S(1)}, s32[16]{0:T(128)}, u32[]{:S(2)}) copy-start(s32[16]{0:T(128)} %param.16) | copy-start | bytes 196
  194.2 11.3 %copy-start.3 = (bf16[1,16,128,512]{3,2,0,1:T(8,128)(2,1)}, bf16[1,16,128,512]{3,2,0,1:T(8,128)(2,1)S(1)}, u32[]{:S(2)}) copy-start(bf16[1,16,128,512]{3,2,0,1:T(8,128)(2,1)S(1)} %all-to-all-done.1) | copy-start | bytes 6291460
  194.2 30.0 %all-to-all-start.3 = ((bf16[16,20,1024]{2,1,0:T(8,128)(2,1)}), bf16[16,20,1024]{2,1,0:T(8,128)(2,1)}, u32[]{:S(2)}, u32[]{:S(2)}) async-start(bf16[16,20,1024]{2,1,0:T(8,128)(2,1)} %all_to_all.76), calls=%async_computation.3 | async-start | bytes 1572864 | tf_op jit(solution)/shard_map/all_to_all | solution.py:95
  224.2 52.7 %copy-start.1 = (bf16[1,16,128,512]{3,2,0,1:T(8,128)(2,1)S(1)}, bf16[1,16,128,512]{3,2,0,1:T(8,128)(2,1)}, u32[]{:S(2)}) copy-start(bf16[1,16,128,512]{3,2,0,1:T(8,128)(2,1)} %get-tuple-element.11) | copy-start | bytes 6291460
  329.0 60.1 %all-to-all-start.2 = ((bf16[1,16,128,512]{3,2,0,1:T(8,128)(2,1)}), bf16[1,16,128,512]{3,2,0,1:T(8,128)(2,1)}, u32[]{:S(2)}, u32[]{:S(2)}) async-start(bf16[1,16,128,512]{3,2,0,1:T(8,128)(2,1)} %get-tuple-element.12), calls=%async_computation.2 | async-start | bytes 4194304 | tf_op jit(solution)/shard_map/all_to_all | solution.py:14
  334.2 28.5 %all-gather.5.cloned.1.call-start = ((), (), s32[]{:S(2)}) async-start(), calls=%async_computation.11 | async-start | bytes 1966080 | tf_op jit(solution)/shard_map/all_gather | solution.py:99
  336.3 52.8 %all-gather.3.cloned.1.call-start = ((), (), s32[]{:S(2)}) async-start(), calls=%async_computation.10 | async-start | bytes 1966080 | tf_op jit(solution)/shard_map/all_gather | solution.py:100
  337.4 81.6 %reduce-scatter.2.cloned.1.call-start = ((), (), s32[]{:S(2)}) async-start(), calls=%async_computation.12 | async-start | bytes 1966080 | tf_op jit(solution)/shard_map/reduce_scatter | solution.py:106
  362.7 3.8 copy-start
  389.1 3.5 copy-start.2
  392.5 0.9 copy-start.4
  392.6 0.9 copy-start.7
  395.5 31.2 %copy-start.8 = (bf16[320,512]{1,0:T(8,128)(2,1)S(1)}, bf16[320,512]{1,0:T(8,128)(2,1)}, u32[]{:S(2)}) copy-start(bf16[320,512]{1,0:T(8,128)(2,1)} %copy-done.7) | copy-start | bytes 983044
  420.9 24.3 %all-to-all-start.8 = ((bf16[16,20,1024]{2,1,0:T(8,128)(2,1)}), bf16[16,20,1024]{2,1,0:T(8,128)(2,1)S(1)}, u32[]{:S(2)}, u32[]{:S(2)}) async-start(bf16[16,20,1024]{2,1,0:T(8,128)(2,1)} %all_to_all.85), calls=%async_computation.9 | async-start | bytes 1572864 | tf_op jit(solution)/shard_map/all_to_all | solution.py:109
  426.7 3.3 copy-start.5
  430.0 3.3 copy-start.11
  430.0 3.3 copy-start.12
  430.0 3.3 copy-start.13
Sparse Core Ops, SparseCore 0:
  337.2 25.4 all-gather.4
  364.8 24.2 all-gather.2
  395.6 23.2 reduce-scatter.1
where the time goes:
time: 455 us; the launch traced here: 454 us
  blocking collectives  236 us (52%)
  waiting for transfers between devices  116 us (25%)
  local copies, waits for them, and re-layouts  28.3 us (6%)
  starting transfers between devices  27.5 us (6%)
  matrix products  21.8 us (5%)
  between operations  14 us (3%)
  other arithmetic  9.94 us (2%)
    all_to_all x2, blocking collectives, relay_weights(): lax.all_to_all(second, 'expert', split_axis=1, concat_axis=0, tiled=True)  105 us
    all_to_all x2, blocking collectives, relay_weights(): lax.all_to_all(first, 'expert', split_axis=1, concat_axis=0, tiled=True)  104 us
    all_to_all x2, waiting for transfers between devices, relay_weights(): lax.all_to_all(third, 'expert', split_axis=1, concat_axis=0, tiled=True)  34.2 us
    all_to_all x1, blocking collectives, local(): lax.all_to_all(grads, 'expert', split_axis=0, concat_axis=0, tiled=True)  27.3 us
    all_gather x1, waiting for transfers between devices, local(): lax.all_gather(part_in, 'dp', axis=1, tiled=True)  25.3 us
    reduce_scatter x1, waiting for transfers between devices, local(): lax.psum_scatter(partial_value, 'dp', scatter_dimension=1, tiled=True)  23.4 us
    all_gather x1, waiting for transfers between devices, local(): lax.all_gather(part_out, 'dp', axis=1, tiled=True)  20.9 us
    all_to_all x1, starting transfers between devices, local(): lax.all_to_all(inputs, 'expert', split_axis=0, concat_axis=0, tiled=True)  11.3 us
  transfers between devices with their start and end apart: 7, of which 6 were waited for; matrix products, arithmetic and copies ran while one was open for 8% of the time, Pallas kernels for 0%

commit v1 on v0

v1 whole, which is shorter than its diff:
```python
import jax
import jax.numpy as jnp
from jax import lax
from jax.sharding import PartitionSpec as P

contract_rows = (((0,), (0,)), ((), ()))
contract_cols = (((1,), (1,)), ((), ()))


def pair_rows(cotangent, routes, probs, expert):
    weight = jnp.sum(jnp.where(routes == expert, probs, 0.0), axis=1)
    return (cotangent.astype(jnp.float32) * weight[:, None]).astype(jnp.bfloat16)


def local(tokens, cotangent, routes, probs, matching, gate_weight, up_weight, down_weight):
    experts = matching.shape[0]
    tok_rows = routes.shape[0]
    hidden_width = gate_weight.shape[2]
    me = lax.axis_index("expert")
    w_gate, w_up, w_down = gate_weight[0], up_weight[0], down_weight[0]
    routes_all = lax.all_gather(routes, "expert", axis=0, tiled=True)
    probs_all = lax.all_gather(probs, "expert", axis=0, tiled=True)
    both = jnp.stack([tokens, cotangent], axis=0)
    both = lax.all_gather(both, "dp", axis=2, tiled=True)
    both = lax.all_gather(both, "expert", axis=1, tiled=True)
    rows, cot = both[0], both[1]
    grads = pair_rows(cot, routes_all, probs_all, me)
    gate = jnp.dot(rows, w_gate, preferred_element_type=jnp.float32)
    upper = jnp.dot(rows, w_up, preferred_element_type=jnp.float32)
    sig = jax.nn.sigmoid(gate)
    hidden = (gate * sig * upper).astype(jnp.bfloat16)
    hidden_back = jnp.dot(grads, w_down, preferred_element_type=jnp.float32)
    up_back = (hidden_back * gate * sig).astype(jnp.bfloat16)
    gate_back = (hidden_back * upper * sig * (1.0 + gate * (1.0 - sig))).astype(jnp.bfloat16)
    packed = jnp.concatenate([gate_back, up_back, hidden], axis=1)
    packed = packed.reshape(experts, tok_rows, 3 * hidden_width)
    spread = lax.all_to_all(packed, "expert", split_axis=0, concat_axis=0, tiled=True)
    ordered = jnp.take(spread, matching, axis=0)
    landed = lax.all_to_all(ordered, "expert", split_axis=0, concat_axis=0, tiled=True)
    landed = landed.reshape(experts * tok_rows, 3 * hidden_width)
    part = lax.dot_general(gate_back, w_gate, contract_cols, preferred_element_type=jnp.float32)
    part = part + lax.dot_general(up_back, w_up, contract_cols, preferred_element_type=jnp.float32)
    part = part.astype(jnp.bfloat16)
    summed = lax.psum_scatter(part, "dp", scatter_dimension=1, tiled=True)
    summed = summed.reshape(experts, tok_rows, summed.shape[1])
    back = lax.all_to_all(summed, "expert", split_axis=0, concat_axis=0, tiled=True)
    input_grad = jnp.sum(back.astype(jnp.float32), axis=0).astype(jnp.bfloat16)
    partner = matching[me]
    p_grads = pair_rows(cot, routes_all, probs_all, partner)
    g_gate = lax.dot_general(
        rows, landed[:, :hidden_width], contract_rows, preferred_element_type=jnp.float32
    )
    g_up = lax.dot_general(
        rows, landed[:, hidden_width : 2 * hidden_width], contract_rows, preferred_element_type=jnp.float32
    )
    g_down = lax.dot_general(
        p_grads, landed[:, 2 * hidden_width :], contract_rows, preferred_element_type=jnp.float32
    )
    return (
        input_grad,
        g_gate[None],
        g_up[None],
        g_down[None],
    )


def solution(mesh):
    placed = (
        P("expert", "dp"),
        P("expert", "dp"),
        P("expert", None),
        P("expert", None),
        P(),
        P("expert", None, "dp"),
        P("expert", None, "dp"),
        P("expert", None, "dp"),
    )
    return jax.shard_map(
        local,
        mesh=mesh,
        in_specs=placed,
        out_specs=(
            P("expert", "dp"),
            P("expert", None, "dp"),
            P("expert", None, "dp"),
            P("expert", None, "dp"),
        ),
        check_vma=False,
    )
```

time: 455 us -> 204 us (0.45)
  blocking collectives: 236 us -> 48.2 us
  waiting for transfers between devices: 116 us -> 75.6 us
  local copies, waits for them, and re-layouts: 28.3 us -> 8.26 us
  starting transfers between devices: 27.5 us -> 22.7 us
    all_to_all x5 -> x0, blocking collectives: 236 us -> none  [the longest x2 105 us: relay_weights(): lax.all_to_all(second, 'expert', split_axis=1, concat_axis=0, tiled=True)]
    all_gather x0 -> x3, blocking collectives: none -> 48.2 us  [the longest x1 22.6 us: local(): routes_all = lax.all_gather(routes, 'expert', axis=0, tiled=True)]
    all_gather x2 -> x1, waiting for transfers between devices: 46.2 us -> 9.22 us  [local(): both = lax.all_gather(both, 'expert', axis=1, tiled=True)]
    reduce_scatter x1, waiting for transfers between devices: 23.4 us -> 0.02 us  [local(): summed = lax.psum_scatter(part, 'dp', scatter_dimension=1, tiled=True)]
    all_to_all x4 -> x3, waiting for transfers between devices: 46.7 us -> 66.3 us  [the longest x1 31.9 us: local(): lax.all_to_all(ordered, 'expert', split_axis=0, concat_axis=0, tiled=True)]
    gather x6 -> x1, local copies, waits for them, and re-layouts: 15.2 us -> 3.2 us  [local(): ordered = jnp.take(spread, matching, axis=0)]
    all_to_all x5 -> x0, local copies, waits for them, and re-layouts: 7.17 us -> none  [the longest x2 4.05 us: local(): lax.all_to_all(inputs, 'expert', split_axis=0, concat_axis=0, tiled=True)]
    reshape x1 -> x0, other arithmetic: 5.19 us -> none  [migrate(): jnp.take(s, matching, axis=0).reshape(1, experts, piece_rows, hidden_width)]
  transfers between devices with their start and end apart: 7 -> 5, of which waited for: 6 -> 4; matrix products, arithmetic and copies ran while one was open for 8% -> 14% of each run, Pallas kernels for 0% -> 0%
where the time goes in v1:
time: 204 us; the launch traced here: 202 us
  waiting for transfers between devices  75.6 us (37%)
  blocking collectives  48.2 us (24%)
  matrix products  26.2 us (13%)
  starting transfers between devices  22.7 us (11%)
  between operations  14.2 us (7%)
  local copies, waits for them, and re-layouts  8.26 us (4%)
  other arithmetic  6.57 us (3%)
    all_to_all x1, waiting for transfers between devices, local(): lax.all_to_all(ordered, 'expert', split_axis=0, concat_axis=0, tiled=True)  31.9 us
    all_to_all x1, waiting for transfers between devices, local(): lax.all_to_all(packed, 'expert', split_axis=0, concat_axis=0, tiled=True)  25.6 us
    all_gather x1, blocking collectives, local(): routes_all = lax.all_gather(routes, 'expert', axis=0, tiled=True)  22.6 us
    all_gather x1, blocking collectives, local(): probs_all = lax.all_gather(probs, 'expert', axis=0, tiled=True)  18.5 us
    all_gather x1, waiting for transfers between devices, local(): both = lax.all_gather(both, 'expert', axis=1, tiled=True)  9.22 us
    all_to_all x1, starting transfers between devices, local(): lax.all_to_all(ordered, 'expert', split_axis=0, concat_axis=0, tiled=True)  9.14 us
    all_to_all x1, starting transfers between devices, local(): lax.all_to_all(summed, 'expert', split_axis=0, concat_axis=0, tiled=True)  9.11 us
    all_to_all x1, waiting for transfers between devices, local(): lax.all_to_all(summed, 'expert', split_axis=0, concat_axis=0, tiled=True)  8.85 us
  transfers between devices with their start and end apart: 5, of which 4 were waited for; matrix products, arithmetic and copies ran while one was open for 14% of the time, Pallas kernels for 0%

profile of v1, /device:TPU:0, one launch (start us, length us, event | category | flops | bytes accessed | tf_op | source)
XLA Modules:
  0.0 201.7 jit_solution(15081266872429991125)
XLA Ops:
  7.2 1.0 pad_maximum_fusion.1
  8.3 7.2 %all_gather.12 = bf16[2,32,2048]{2,1,0:T(8,128)(2,1)} all-gather(bf16[2,32,1024]{2,1,0:T(8,128)(2,1)S(1)} %pad_maximum_fusion.1), channel_id=1, replica_groups=mesh['dp'=2,'expert'=16] {'dp'}, dimensions={2}, use_global_device_ids=true | all-gather | bytes 393216 | tf_op jit(solution)/shard_map/all_gather | solution.py:24
  15.5 1.2 dynamic_slice.3
  16.7 22.6 %all-gather = s32[16,32,8]{1,2,0:T(8,128)S(1)} all-gather(s32[1,32,8]{1,2,0:T(8,128)} %bitcast.53), channel_id=1, replica_groups=mesh['dp'=2,'expert'=16] {'expert'}, dimensions={0}, use_global_device_ids=true | all-gather | bytes 17408 | tf_op jit(solution)/shard_map/all_gather | solution.py:21
  39.3 18.5 %all-gather.1 = f32[16,32,8]{1,2,0:T(8,128)S(1)} all-gather(f32[1,32,8]{1,2,0:T(8,128)} %bitcast.54), channel_id=1, replica_groups=mesh['dp'=2,'expert'=16] {'expert'}, dimensions={0}, use_global_device_ids=true | all-gather | bytes 17408 | tf_op jit(solution)/shard_map/all_gather | solution.py:22
  58.6 9.2 %all-gather.4.cloned.1.call-done = bf16[2,512,2048]{2,1,0:T(8,128)(2,1)} async-done(((bf16[2,32,2048]{2,1,0:T(8,128)(2,1)}), bf16[2,512,2048]{2,1,0:T(8,128)(2,1)}) %all-gather.4.cloned.1.call-update) | async-done | bytes 4194320 | tf_op jit(solution)/shard_map/all_gather | solution.py:25
  67.8 3.7 %fusion.9 = f32[512,512]{0,1:T(8,128)S(1)} fusion(bf16[1,2048,512]{2,1,0:T(8,128)(2,1)} %param.13, bf16[2,512,2048]{2,1,0:T(8,128)(2,1)} %all-gather.4.cloned.1.call-done), kind=kOutput, calls=%fused_computation.15 | convolution fusion | flops 1073741824 | bytes 5242880 | tf_op jit(solution)/shard_map/dot_general | solution.py:28
  71.9 1.4 fusion.5
  73.3 1.7 multiply_convert_fusion
  75.0 1.2 pad_maximum_fusion
  76.2 2.6 %copy.13 = bf16[512,1536]{1,0:T(8,128)(2,1)} copy(bf16[512,1536]{0,1:T(8,128)(2,1)} %pad_maximum_fusion) | data formatting | bytes 3145728 | tf_op jit(solution)/shard_map/concatenate | solution.py:35
  78.8 4.4 %all-to-all-start.1 = ((bf16[16,32,1536]{2,1,0:T(8,128)(2,1)}), bf16[16,32,1536]{2,1,0:T(8,128)(2,1)}, u32[]{:S(2)}, u32[]{:S(2)}) async-start(bf16[16,32,1536]{2,1,0:T(8,128)(2,1)} %bitcast.49), calls=%async_computation.2 | async-start | bytes 3145728 | tf_op jit(solution)/shard_map/all_to_all | solution.py:37
  83.3 2.9 %fusion.7 = f32[512,2048]{1,0:T(8,128)S(1)} fusion(bf16[512,512]{0,1:T(8,128)(2,1)S(1)} %get-tuple-element.7, bf16[1,2048,512]{2,1,0:T(8,128)(2,1)} %param.13), kind=kOutput, calls=%fused_computation.13 | convolution fusion | flops 1073741824 | bytes 6815744 | tf_op jit(solution)/shard_map/dot_general | solution.py:41
  86.2 2.6 %add_convert_fusion = bf16[512,2048]{1,0:T(8,128)(2,1)} fusion(f32[512,2048]{1,0:T(8,128)S(1)} %fusion.7, bf16[512,512]{0,1:T(8,128)(2,1)S(1)} %get-tuple-element.8, bf16[1,2048,512]{2,1,0:T(8,128)(2,1)S(1)} %copy-done), kind=kOutput, calls=%fused_computation.6 | convolution fusion | flops 1075838976 | bytes 8912896 | tf_op jit(solution)/shard_map/dot_general | solution.py:42
  89.5 25.6 %all-to-all-done.1 = bf16[16,32,1536]{2,1,0:T(8,128)(2,1)} async-done(((bf16[16,32,1536]{2,1,0:T(8,128)(2,1)}), bf16[16,32,1536]{2,1,0:T(8,128)(2,1)}, u32[]{:S(2)}, u32[]{:S(2)}) %all-to-all-start.1) | async-done | bytes 1572896 | tf_op jit(solution)/shard_map/all_to_all | solution.py:37
  115.1 3.2 %gather_fusion = bf16[16,32,1536]{2,1,0:T(8,128)(2,1)} fusion(bf16[16,32,1536]{2,1,0:T(8,128)(2,1)} %all-to-all-done.1, s32[1024]{0:T(1024)S(1)} %pad_clamp_fusion), kind=kCustom, calls=%fused_computation | custom fusion | bytes 3145792 | tf_op jit(solution)/shard_map/jit(_take)/gather | solution.py:38
  118.3 2.8 %broadcast_select_fusion = bf16[16,32,1536]{2,1,0:T(8,128)(2,1)} fusion(bf16[16,32,1536]{2,1,0:T(8,128)(2,1)} %gather_fusion, pred[16]{0:T(512)(128)(4,1)S(1)} %compare_and_fusion), kind=kLoop, calls=%fused_computation.26 | loop fusion | flops 786432 | bytes 3145744 | tf_op jit(solution)/shard_map/jit(_take)/select_n | solution.py:38
  121.0 9.1 %all-to-all-start.2 = ((bf16[16,32,1536]{2,1,0:T(8,128)(2,1)}), bf16[16,32,1536]{2,1,0:T(8,128)(2,1)}, u32[]{:S(2)}, u32[]{:S(2)}) async-start(bf16[16,32,1536]{2,1,0:T(8,128)(2,1)} %broadcast_select_fusion), calls=%async_computation.3 | async-start | bytes 3145728 | tf_op jit(solution)/shard_map/all_to_all | solution.py:39
  130.2 31.9 %all-to-all-done.2 = bf16[16,32,1536]{2,1,0:T(8,128)(2,1)} async-done(((bf16[16,32,1536]{2,1,0:T(8,128)(2,1)}), bf16[16,32,1536]{2,1,0:T(8,128)(2,1)}, u32[]{:S(2)}, u32[]{:S(2)}) %all-to-all-start.2) | async-done | bytes 1572896 | tf_op jit(solution)/shard_map/all_to_all | solution.py:39
  162.1 9.1 %all-to-all-start = ((bf16[16,32,1024]{2,1,0:T(8,128)(2,1)}), bf16[16,32,1024]{2,1,0:T(8,128)(2,1)S(1)}, u32[]{:S(2)}, u32[]{:S(2)}) async-start(bf16[16,32,1024]{2,1,0:T(8,128)(2,1)} %bitcast.50), calls=%async_computation.1 | async-start | bytes 2097152 | tf_op jit(solution)/shard_map/all_to_all | solution.py:46
  171.3 5.1 %convolution_bitcast_fusion.1 = f32[1,2048,512]{2,1,0:T(8,128)} fusion(bf16[2,512,2048]{2,1,0:T(8,128)(2,1)} %all-gather.4.cloned.1.call-done, bf16[512,1536]{1,0:T(8,128)(2,1)} %bitcast.11), kind=kOutput, calls=%fused_computation.8 | convolution fusion | flops 1073741824 | bytes 6815744 | tf_op jit(solution)/shard_map/dot_general | solution.py:53
  176.4 4.4 %convolution_bitcast_fusion.2 = f32[1,2048,512]{2,1,0:T(8,128)} fusion(bf16[2,512,2048]{2,1,0:T(8,128)(2,1)S(1)} %copy-done.2, bf16[512,1536]{1,0:T(8,128)(2,1)} %bitcast.11), kind=kOutput, calls=%fused_computation.9 | convolution fusion | flops 1073741824 | bytes 6815744 | tf_op jit(solution)/shard_map/dot_general | solution.py:50
  180.8 4.5 %convolution_bitcast_fusion = f32[1,2048,512]{2,1,0:T(8,128)} fusion(f32[512]{0:T(512)S(1)} %reshape.58, bf16[2,512,2048]{2,1,0:T(8,128)(2,1)S(1)} %copy-done.2, bf16[512,1536]{1,0:T(8,128)(2,1)} %bitcast.11), kind=kOutput, calls=%fused_computation.7 | convolution fusion | flops 1076887552 | bytes 6817792 | tf_op jit(solution)/shard_map/dot_general | solution.py:56
  185.2 8.9 %all-to-all-done = bf16[16,32,1024]{2,1,0:T(8,128)(2,1)S(1)} async-done(((bf16[16,32,1024]{2,1,0:T(8,128)(2,1)}), bf16[16,32,1024]{2,1,0:T(8,128)(2,1)S(1)}, u32[]{:S(2)}, u32[]{:S(2)}) %all-to-all-start) | async-done | bytes 1048608 | tf_op jit(solution)/shard_map/all_to_all | solution.py:46
  (22 shorter events, 2.9 us)
Async XLA Ops:
  7.2 66.2 %copy-start = (bf16[1,2048,512]{2,1,0:T(8,128)(2,1)S(1)}, bf16[1,2048,512]{2,1,0:T(8,128)(2,1)}, u32[]{:S(2)}) copy-start(bf16[1,2048,512]{2,1,0:T(8,128)(2,1)} %param.14) | copy-start | bytes 6291460
  7.2 60.6 %all-gather.4.cloned.1.call-start = ((), (), s32[]{:S(2)}) async-start(), calls=%async_computation.4 | async-start | bytes 4456448 | tf_op jit(solution)/shard_map/all_gather | solution.py:25
  67.8 3.7 %copy-start.1 = (bf16[2,512,2048]{2,1,0:T(8,128)(2,1)S(1)}, bf16[2,512,2048]{2,1,0:T(8,128)(2,1)}, u32[]{:S(2)}) copy-start(bf16[2,512,2048]{2,1,0:T(8,128)(2,1)} %all-gather.4.cloned.1.call-done) | copy-start | bytes 12582916
  67.8 4.1 %copy-start.3 = (bf16[1,2048,512]{2,1,0:T(8,128)(2,1)S(1)}, bf16[1,2048,512]{2,1,0:T(8,128)(2,1)}, u32[]{:S(2)}) copy-start(bf16[1,2048,512]{2,1,0:T(8,128)(2,1)} %param.15) | copy-start | bytes 6291460
  78.8 36.2 %all-to-all-start.1 = ((bf16[16,32,1536]{2,1,0:T(8,128)(2,1)}), bf16[16,32,1536]{2,1,0:T(8,128)(2,1)}, u32[]{:S(2)}, u32[]{:S(2)}) async-start(bf16[16,32,1536]{2,1,0:T(8,128)(2,1)} %bitcast.49), calls=%async_computation.2 | async-start | bytes 3145728 | tf_op jit(solution)/shard_map/all_to_all | solution.py:37
  83.2 47.0 %reduce-scatter.2.cloned.1.call-start = ((), (), s32[]{:S(2)}) async-start(), calls=%async_computation.5 | async-start | bytes 3145728 | tf_op jit(solution)/shard_map/reduce_scatter | solution.py:44
  88.8 0.7 copy-start.4
  121.0 41.1 %all-to-all-start.2 = ((bf16[16,32,1536]{2,1,0:T(8,128)(2,1)}), bf16[16,32,1536]{2,1,0:T(8,128)(2,1)}, u32[]{:S(2)}, u32[]{:S(2)}) async-start(bf16[16,32,1536]{2,1,0:T(8,128)(2,1)} %broadcast_select_fusion), calls=%async_computation.3 | async-start | bytes 3145728 | tf_op jit(solution)/shard_map/all_to_all | solution.py:39
  162.1 32.0 %all-to-all-start = ((bf16[16,32,1024]{2,1,0:T(8,128)(2,1)}), bf16[16,32,1024]{2,1,0:T(8,128)(2,1)S(1)}, u32[]{:S(2)}, u32[]{:S(2)}) async-start(bf16[16,32,1024]{2,1,0:T(8,128)(2,1)} %bitcast.50), calls=%async_computation.1 | async-start | bytes 2097152 | tf_op jit(solution)/shard_map/all_to_all | solution.py:46
  171.3 5.1 %copy-start.2 = (bf16[2,512,2048]{2,1,0:T(8,128)(2,1)S(1)}, bf16[2,512,2048]{2,1,0:T(8,128)(2,1)}, u32[]{:S(2)}) copy-start(bf16[2,512,2048]{2,1,0:T(8,128)(2,1)} %all-gather.4.cloned.1.call-done) | copy-start | bytes 12582916
Sparse Core Ops, SparseCore 0:
  15.6 52.1 all-gather.3
  89.0 33.1 reduce-scatter.1

commit v2 on v1

v2 whole, which is shorter than its diff:
```python
import functools

import jax
import jax.numpy as jnp
from jax import lax
from jax.experimental import pallas as pl
from jax.experimental.pallas import tpu as pltpu
from jax.sharding import PartitionSpec as P

contract_rows = (((0,), (0,)), ((), ()))
contract_cols = (((1,), (1,)), ((), ()))
MESH = pl.DeviceIdType.MESH


def bit_count(size):
    return size.bit_length() - 1


def flipped(index, bit):
    step = 2**bit
    return index + step * (1 - 2 * ((index // step) % 2))


def gather_orders(expert_bits, dp_bits):
    far = [("expert", b) for b in range(expert_bits - 1, 1, -1)]
    mid = [("expert", 1)]
    last = [("expert", 0)]
    across = [("dp", b) for b in range(dp_bits)]
    return (far + across + mid + last, far + mid + across + last, far + mid + last)


def gather_kernel(
    n_expert, n_dp, tokens, cotangent, table, all_tokens, all_cotangent, all_table, send, recv, own
):
    e = lax.axis_index("expert")
    d = lax.axis_index("dp")
    expert_bits, dp_bits = bit_count(n_expert), bit_count(n_dp)
    width = tokens.shape[1]
    half = tokens.shape[0] // 2

    def peer(axis, bit):
        if axis == "expert":
            return (d, flipped(e, bit))
        return (flipped(d, bit), e)

    def held(ref, done, rows, data):
        where = []
        for b in range(expert_bits - 1, -1, -1):
            where.append(slice(None) if ("expert", b) in done else (e // 2**b) % 2)
        where.append(rows)
        if data:
            k = len([x for x in done if x[0] == "dp"])
            start = pl.multiple_of((d // 2**k) * (2**k * width), width)
            where.append(pl.ds(start, 2**k * width))
        else:
            where.append(slice(None))
        return ref.at[tuple(where)]

    barrier = pltpu.get_barrier_semaphore()
    links = [("expert", b) for b in range(expert_bits)] + [("dp", b) for b in range(dp_bits)]
    for link in links:
        pl.semaphore_signal(barrier, inc=1, device_id=peer(*link), device_id_type=MESH)

    first, second, plain = gather_orders(expert_bits, dp_bits)
    top, low, whole = pl.ds(0, half), pl.ds(half, half), pl.ds(0, 2 * half)
    parts = [
        (tokens, all_tokens, top, first, True),
        (tokens, all_tokens, low, second, True),
        (cotangent, all_cotangent, top, first, True),
        (cotangent, all_cotangent, low, second, True),
        (table, all_table, whole, plain, False),
    ]
    locals_ = []
    for i, (src, dst, rows, order, data) in enumerate(parts):
        c = pltpu.make_async_copy(src.at[rows], held(dst, [], rows, data), own.at[i])
        c.start()
        locals_.append(c)
    pl.semaphore_wait(barrier, len(links))
    flights = [[] for _ in parts]
    steps = max(len(p[3]) for p in parts)
    for s in range(steps):
        for i, (src, dst, rows, order, data) in enumerate(parts):
            if s >= len(order):
                continue
            if s == 0:
                locals_[i].wait()
            else:
                flights[i][s - 1].wait_recv()
            block = held(dst, order[:s], rows, data)
            c = pltpu.make_async_remote_copy(
                src_ref=block,
                dst_ref=block,
                send_sem=send.at[i, s],
                recv_sem=recv.at[i, s],
                device_id=peer(*order[s]),
                device_id_type=MESH,
            )
            c.start()
            flights[i].append(c)
    for f in flights:
        f[-1].wait_recv()
        for c in f:
            c.wait_send()


def gather_all(n_expert, n_dp, tokens, cotangent, table):
    lead = (2,) * bit_count(n_expert)
    rows, width = tokens.shape
    steps = bit_count(n_expert) + bit_count(n_dp)
    wide = jax.ShapeDtypeStruct(lead + (rows, width * n_dp), tokens.dtype)
    small = jax.ShapeDtypeStruct(lead + table.shape, table.dtype)
    outs = pl.pallas_call(
        functools.partial(gather_kernel, n_expert, n_dp),
        out_shape=(wide, wide, small),
        in_specs=[pl.BlockSpec(memory_space=pltpu.VMEM)] * 3,
        out_specs=[pl.BlockSpec(memory_space=pl.ANY)] * 3,
        scratch_shapes=[
            pltpu.SemaphoreType.DMA((5, steps)),
            pltpu.SemaphoreType.DMA((5, steps)),
            pltpu.SemaphoreType.DMA((5,)),
        ],
        compiler_params=pltpu.CompilerParams(collective_id=0, has_side_effects=True),
    )(tokens, cotangent, table)
    total = n_expert * rows
    return (
        outs[0].reshape(total, width * n_dp),
        outs[1].reshape(total, width * n_dp),
        outs[2].reshape(total, table.shape[1]),
    )


def column(table, index):
    lanes = lax.broadcasted_iota(jnp.int32, table.shape, 1)
    return jnp.sum(jnp.where(lanes == index, table, 0.0), axis=1)


def scaled(cotangent, weight):
    return (cotangent.astype(jnp.float32) * weight[:, None]).astype(jnp.bfloat16)


def selector(weight, blocks, capacity, kinds, slots):
    chosen = (weight > 0.0).reshape(blocks, -1)
    tok_rows = chosen.shape[1]
    at = lax.broadcasted_iota(jnp.int32, (tok_rows, tok_rows), 0)
    to = lax.broadcasted_iota(jnp.int32, (tok_rows, tok_rows), 1)
    upto = jnp.where(at <= to, 1.0, 0.0).astype(jnp.bfloat16)
    rank = jnp.dot(chosen.astype(jnp.bfloat16), upto, preferred_element_type=jnp.float32)
    rank = jnp.where(chosen, rank.astype(jnp.int32) - 1, -1)
    wide = jnp.concatenate([rank] * kinds, axis=1)[:, None, :]
    shape = (blocks, slots, kinds * tok_rows)
    slot = lax.broadcasted_iota(jnp.int32, shape, 1)
    kind = lax.broadcasted_iota(jnp.int32, shape, 2) // tok_rows
    hit = (wide >= 0) & (wide + kind * capacity == slot)
    return jnp.where(hit, 1.0, 0.0).astype(jnp.bfloat16)


def local(n_expert, n_dp, tokens, cotangent, routes, probs, matching, w_gate, w_up, w_down):
    experts = matching.shape[0]
    tok_rows, top_count = routes.shape
    w_gate, w_up, w_down = w_gate[0], w_up[0], w_down[0]
    hidden_width = w_gate.shape[1]
    capacity = max(2, 5 * tok_rows * top_count // (4 * experts))
    slots = -(-3 * capacity // 16) * 16
    me = lax.axis_index("expert")
    lanes = -(-experts // 128) * 128
    names = jnp.arange(lanes, dtype=jnp.int32)
    table = jnp.sum(
        jnp.where(routes[:, :, None] == names[None, None, :], probs[:, :, None], 0.0), axis=1
    )
    rows, cot, table = gather_all(n_expert, n_dp, tokens, cotangent, table)
    weight = column(table, me)
    grads = scaled(cot, weight)
    gate = jnp.dot(rows, w_gate, preferred_element_type=jnp.float32)
    upper = jnp.dot(rows, w_up, preferred_element_type=jnp.float32)
    sig = jax.nn.sigmoid(gate)
    hidden = (gate * sig * upper).astype(jnp.bfloat16)
    hidden_back = jnp.dot(grads, w_down, preferred_element_type=jnp.float32)
    up_back = (hidden_back * gate * sig).astype(jnp.bfloat16)
    gate_back = (hidden_back * upper * sig * (1.0 + gate * (1.0 - sig))).astype(jnp.bfloat16)
    cubes = [v.reshape(experts, tok_rows, hidden_width) for v in (gate_back, up_back, hidden)]
    stacked = jnp.concatenate(cubes, axis=1)
    pick = selector(weight, experts, capacity, 3, slots)
    packed = jnp.einsum(
        "jrt,jth->jrh", pick, stacked, preferred_element_type=jnp.float32
    ).astype(jnp.bfloat16)
    spread = lax.all_to_all(packed, "expert", split_axis=0, concat_axis=0, tiled=True)
    ordered = jnp.take(spread, matching, axis=0)
    landed = lax.all_to_all(ordered, "expert", split_axis=0, concat_axis=0, tiled=True)
    part = lax.dot_general(gate_back, w_gate, contract_cols, preferred_element_type=jnp.float32)
    part = part + lax.dot_general(up_back, w_up, contract_cols, preferred_element_type=jnp.float32)
    part = part.astype(jnp.bfloat16)
    summed = lax.psum_scatter(part, "dp", scatter_dimension=1, tiled=True)
    summed = summed.reshape(experts, tok_rows, summed.shape[1])
    back = lax.all_to_all(summed, "expert", split_axis=0, concat_axis=0, tiled=True)
    input_grad = jnp.sum(back.astype(jnp.float32), axis=0).astype(jnp.bfloat16)
    p_weight = column(table, matching[me])
    p_pick = selector(p_weight, experts, capacity, 3, slots)
    dense = jnp.einsum(
        "jrt,jrh->jth", p_pick, landed, preferred_element_type=jnp.float32
    ).astype(jnp.bfloat16)
    p_grads = scaled(cot, p_weight)
    total = experts * tok_rows

    def take(kind):
        return dense[:, kind * tok_rows : (kind + 1) * tok_rows].reshape(total, hidden_width)

    g_gate = lax.dot_general(rows, take(0), contract_rows, preferred_element_type=jnp.float32)
    g_up = lax.dot_general(rows, take(1), contract_rows, preferred_element_type=jnp.float32)
    g_down = lax.dot_general(p_grads, take(2), contract_rows, preferred_element_type=jnp.float32)
    return (input_grad, g_gate[None], g_up[None], g_down[None])


def solution(mesh):
    weights = P("expert", None, "dp")
    return jax.shard_map(
        functools.partial(local, mesh.shape["expert"], mesh.shape["dp"]),
        mesh=mesh,
        in_specs=(
            P("expert", "dp"),
            P("expert", "dp"),
            P("expert", None),
            P("expert", None),
            P(),
            weights,
            weights,
            weights,
        ),
        out_specs=(P("expert", "dp"), weights, weights, weights),
        check_vma=False,
    )
```

time: 204 us -> 162 us (0.79)
  blocking collectives: 48.2 us -> 0 us
  Pallas kernels: 0 us -> 39.3 us
  waiting for transfers between devices: 75.6 us -> 48.7 us
  starting transfers between devices: 22.7 us -> 17.9 us
  matrix products: 26.2 us -> 23.1 us
  other arithmetic: 6.57 us -> 8.67 us
    all_gather x3 -> x0, blocking collectives: 48.2 us -> none  [the longest x1 22.6 us: local(): routes_all = lax.all_gather(routes, 'expert', axis=0, tiled=True)]
    pallas_call x0 -> x1, Pallas kernels: none -> 39.3 us  [gather_all(): pl.pallas_call(functools.partial(gather_kernel, n_expert, n_dp), out_shap...]
    all_gather x1 -> x0, waiting for transfers between devices: 9.22 us -> none  [local(): both = lax.all_gather(both, 'expert', axis=1, tiled=True)]
    all_to_all x1, waiting for transfers between devices: 31.9 us -> 22.9 us  [local(): lax.all_to_all(ordered, 'expert', split_axis=0, concat_axis=0, tiled=True)]
    all_to_all x1, waiting for transfers between devices: 25.6 us -> 16.7 us  [local(): lax.all_to_all(packed, 'expert', split_axis=0, concat_axis=0, tiled=True)]
    unnamed x10 -> x18, local copies, waits for them, and re-layouts: 1.09 us -> 5.03 us
    convert_element_type x0 -> x1, other arithmetic: none -> 3.78 us  [scaled(): (cotangent.astype(jnp.float32) * weight[:, None]).astype(jnp.bfloat16)]
    concatenate x1 -> x0, local copies, waits for them, and re-layouts: 2.58 us -> none  [local(): packed = jnp.concatenate([gate_back, up_back, hidden], axis=1)]
  transfers between devices with their start and end apart: 5 -> 4, of which waited for: 4 -> 3; matrix products, arithmetic and copies ran while one was open for 14% -> 13% of each run, Pallas kernels for 0% -> 0%
where the time goes in v2:
time: 162 us; the launch traced here: 160 us
  waiting for transfers between devices  48.7 us (30%)
  Pallas kernels  39.3 us (24%)
  matrix products  23.1 us (14%)
  starting transfers between devices  17.9 us (11%)
  between operations  14.2 us (9%)
  other arithmetic  8.67 us (5%)
  local copies, waits for them, and re-layouts  8.31 us (5%)
    pallas_call x1, Pallas kernels, gather_all(): pl.pallas_call(functools.partial(gather_kernel, n_expert, n_dp), out_shap...  39.3 us
    all_to_all x1, waiting for transfers between devices, local(): lax.all_to_all(ordered, 'expert', split_axis=0, concat_axis=0, tiled=True)  22.9 us
    all_to_all x1, waiting for transfers between devices, local(): lax.all_to_all(packed, 'expert', split_axis=0, concat_axis=0, tiled=True)  16.7 us
    all_to_all x1, waiting for transfers between devices, local(): lax.all_to_all(summed, 'expert', split_axis=0, concat_axis=0, tiled=True)  9.18 us
    all_to_all x1, starting transfers between devices, local(): lax.all_to_all(summed, 'expert', split_axis=0, concat_axis=0, tiled=True)  6.8 us
    all_to_all x1, starting transfers between devices, local(): lax.all_to_all(ordered, 'expert', split_axis=0, concat_axis=0, tiled=True)  6.73 us
    unnamed x18, local copies, waits for them, and re-layouts  5.03 us
    all_to_all x1, starting transfers between devices, local(): lax.all_to_all(packed, 'expert', split_axis=0, concat_axis=0, tiled=True)  4.33 us
  transfers between devices with their start and end apart: 4, of which 3 were waited for; matrix products, arithmetic and copies ran while one was open for 13% of the time, Pallas kernels for 0%

profile of v2, /device:TPU:0, one launch (start us, length us, event | category | flops | bytes accessed | tf_op | source)
XLA Modules:
  0.0 160.2 jit_solution(10693991969067717790)
XLA Ops:
  8.9 1.2 dynamic_slice.3
  11.5 39.3 %shard_map.111 = (bf16[2,2,2,2,32,2048]{5,4,3,2,1,0:T(8,128)(2,1)}, bf16[2,2,2,2,32,2048]{5,4,3,2,1,0:T(8,128)(2,1)}, f32[2,2,2,2,32,128]{5,4,3,2,1,0:T(8,128)}) custom-call(bf16[32,1024]{1,0:T(8,128)(2,1)} %tokens.1, bf16[32,1024]{1,0:T(8,128)(2,1)} %cotangent.1, f32[32,128]{1,0:T(8,128)} %select_reduce_fusion.2.table), custom_call_target="tpu_custom_call" | custom-call | tf_op jit(solution)/shard_map/pallas_call | solution.py:112
  50.8 1.2 select_reduce_fusion
  52.4 3.8 %fusion.1 = (bf16[2,2,2,2,32,2048]{5,4,3,2,1,0:T(8,128)(2,1)}, bf16[2,2,2,2,32,2048]{5,4,3,2,1,0:T(8,128)(2,1)S(1)}) fusion(bf16[2,2,2,2,32,2048]{5,4,3,2,1,0:T(8,128)(2,1)} %get-tuple-element.7, f32[2,2,2,2,32]{4,3,2,1,0:T(2,128)S(1)} %get-tuple-element.10, f32[2,2,2,2,32]{4,3,2,1,0:T(2,128)S(1)} %get-tuple-element.11), kind=kLoop, calls=%fused_computation.4 | loop fusion | flops 5242880 | bytes 6295552 | tf_op jit(solution)/shard_map/convert_element_type | solution.py:138
  56.2 1.3 fusion.4
  57.8 1.2 fusion.9
  59.0 1.6 %multiply_convert_fusion = (bf16[512,512]{1,0:T(8,128)(2,1)S(1)}, bf16[512,512]{1,0:T(8,128)(2,1)S(1)}, bf16[512,512]{1,0:T(8,128)(2,1)S(1)}) fusion(f32[512,512]{1,0:T(8,128)S(1)} %fusion.4, f32[512,512]{1,0:T(8,128)S(1)} %fusion.9, bf16[512,2048]{1,0:T(8,128)(2,1)S(1)} %bitcast.55, bf16[1,2048,512]{2,1,0:T(8,128)(2,1)S(1)} %copy-done), kind=kOutput, calls=%fused_computation.32 | convolution fusion | flops 1077936128 | bytes 7864320 | tf_op jit(solution)/shard_map/dot_general | solution.py:174
  60.7 1.4 fusion.17
  62.1 4.3 %all-to-all-start.1 = ((bf16[16,64,512]{2,1,0:T(8,128)(2,1)}), bf16[16,64,512]{2,1,0:T(8,128)(2,1)}, u32[]{:S(2)}, u32[]{:S(2)}) async-start(bf16[16,64,512]{2,1,0:T(8,128)(2,1)} %fusion.17), calls=%async_computation.2 | async-start | bytes 2097152 | tf_op jit(solution)/shard_map/all_to_all | solution.py:186
  66.5 2.9 %fusion.2 = f32[512,2048]{1,0:T(8,128)S(1)} fusion(bf16[512,512]{1,0:T(8,128)(2,1)S(1)} %get-tuple-element.15, bf16[1,2048,512]{2,1,0:T(8,128)(2,1)} %param.13), kind=kOutput, calls=%fused_computation.9 | convolution fusion | flops 1073741824 | bytes 6815744 | tf_op jit(solution)/shard_map/dot_general | solution.py:189
  69.3 2.6 %add_convert_fusion = bf16[512,2048]{1,0:T(8,128)(2,1)} fusion(f32[512,2048]{1,0:T(8,128)S(1)} %fusion.2, bf16[512,512]{1,0:T(8,128)(2,1)S(1)} %get-tuple-element.16, bf16[1,2048,512]{2,1,0:T(8,128)(2,1)S(1)} %copy-done), kind=kOutput, calls=%fused_computation.5 | convolution fusion | flops 1075838976 | bytes 8912896 | tf_op jit(solution)/shard_map/dot_general | solution.py:190
  72.6 16.7 %all-to-all-done.1 = bf16[16,64,512]{2,1,0:T(8,128)(2,1)} async-done(((bf16[16,64,512]{2,1,0:T(8,128)(2,1)}), bf16[16,64,512]{2,1,0:T(8,128)(2,1)}, u32[]{:S(2)}, u32[]{:S(2)}) %all-to-all-start.1) | async-done | bytes 1048608 | tf_op jit(solution)/shard_map/all_to_all | solution.py:186
  89.3 1.8 %gather_fusion = bf16[16,64,512]{2,1,0:T(8,128)(2,1)S(1)} fusion(bf16[16,64,512]{2,1,0:T(8,128)(2,1)} %all-to-all-done.1, s32[1024]{0:T(1024)S(1)} %pad_clamp_fusion), kind=kCustom, calls=%fused_computation | custom fusion | bytes 2097216 | tf_op jit(solution)/shard_map/jit(_take)/gather | solution.py:187
  91.2 1.1 broadcast_select_fusion
  92.3 6.7 %all-to-all-start.2 = ((bf16[16,64,512]{2,1,0:T(8,128)(2,1)}), bf16[16,64,512]{2,1,0:T(8,128)(2,1)S(1)}, u32[]{:S(2)}, u32[]{:S(2)}) async-start(bf16[16,64,512]{2,1,0:T(8,128)(2,1)} %broadcast_select_fusion), calls=%async_computation.3 | async-start | bytes 2097152 | tf_op jit(solution)/shard_map/all_to_all | solution.py:188
  99.1 22.9 %all-to-all-done.2 = bf16[16,64,512]{2,1,0:T(8,128)(2,1)S(1)} async-done(((bf16[16,64,512]{2,1,0:T(8,128)(2,1)}), bf16[16,64,512]{2,1,0:T(8,128)(2,1)S(1)}, u32[]{:S(2)}, u32[]{:S(2)}) %all-to-all-start.2) | async-done | bytes 1048608 | tf_op jit(solution)/shard_map/all_to_all | solution.py:188
  121.9 1.0 copy-done.1
  122.9 6.8 %all-to-all-start = ((bf16[16,32,1024]{2,1,0:T(8,128)(2,1)}), bf16[16,32,1024]{2,1,0:T(8,128)(2,1)S(1)}, u32[]{:S(2)}, u32[]{:S(2)}) async-start(bf16[16,32,1024]{2,1,0:T(8,128)(2,1)} %bitcast.49), calls=%async_computation.1 | async-start | bytes 2097152 | tf_op jit(solution)/shard_map/all_to_all | solution.py:194
  130.0 1.9 %convolution_convert_fusion = bf16[16,96,512]{2,1,0:T(8,128)(2,1)S(1)} fusion(bf16[16,64,512]{2,1,0:T(8,128)(2,1)} %copy-done.1, s32[96]{0:T(128)S(1)} %get-tuple-element.22, s32[96]{0:T(128)S(1)} %get-tuple-element.23, s32[16,96]{1,0:T(8,128)S(1)} %pad_add_fusion, pred[96]{0:T(512)(128)(4,1)S(1)} %compare_and_fusion.1, ...), kind=kOutput, calls=%fused_computation.18 | convolution fusion | flops 102137856 | bytes 2629984 | tf_op jit(solution)/shard_map/jrt,jrh->jth/dot_general | solution.py:198
  132.0 1.4 copy-done.6
  133.4 3.3 %convolution_bitcast_fusion.2 = f32[1,2048,512]{2,1,0:T(8,128)} fusion(bf16[512,2048]{1,0:T(8,128)(2,1)S(1)} %bitcast.56, bf16[512,512]{1,0:T(8,128)(2,1)S(1)} %bitcast.53), kind=kOutput, calls=%fused_computation.8 | convolution fusion | flops 1073741824 | bytes 6815744 | tf_op jit(solution)/shard_map/dot_general | solution.py:207
  136.8 3.3 %convolution_bitcast_fusion.1 = f32[1,2048,512]{2,1,0:T(8,128)} fusion(bf16[512,2048]{1,0:T(8,128)(2,1)S(1)} %bitcast.57, bf16[512,512]{1,0:T(8,128)(2,1)S(1)} %bitcast.52), kind=kOutput, calls=%fused_computation.7 | convolution fusion | flops 1073741824 | bytes 6815744 | tf_op jit(solution)/shard_map/dot_general | solution.py:208
  140.1 3.3 %convolution_bitcast_fusion = f32[1,2048,512]{2,1,0:T(8,128)} fusion(bf16[512,2048]{1,0:T(8,128)(2,1)S(1)} %bitcast.46, bf16[512,512]{1,0:T(8,128)(2,1)S(1)} %bitcast.51), kind=kOutput, calls=%fused_computation.6 | convolution fusion | flops 1073741824 | bytes 6815744 | tf_op jit(solution)/shard_map/dot_general | solution.py:209
  143.4 9.2 %all-to-all-done = bf16[16,32,1024]{2,1,0:T(8,128)(2,1)S(1)} async-done(((bf16[16,32,1024]{2,1,0:T(8,128)(2,1)}), bf16[16,32,1024]{2,1,0:T(8,128)(2,1)S(1)}, u32[]{:S(2)}, u32[]{:S(2)}) %all-to-all-start) | async-done | bytes 1048608 | tf_op jit(solution)/shard_map/all_to_all | solution.py:194
  (38 shorter events, 5.8 us)
Async XLA Ops:
  7.2 51.8 %copy-start = (bf16[1,2048,512]{2,1,0:T(8,128)(2,1)S(1)}, bf16[1,2048,512]{2,1,0:T(8,128)(2,1)}, u32[]{:S(2)}) copy-start(bf16[1,2048,512]{2,1,0:T(8,128)(2,1)} %param.14) | copy-start | bytes 6291460
  52.4 3.8 %copy-start.3 = (bf16[1,2048,512]{2,1,0:T(8,128)(2,1)S(1)}, bf16[1,2048,512]{2,1,0:T(8,128)(2,1)}, u32[]{:S(2)}) copy-start(bf16[1,2048,512]{2,1,0:T(8,128)(2,1)} %param.13) | copy-start | bytes 6291460
  52.4 3.8 %copy-start.5 = (bf16[2,2,2,2,32,2048]{5,4,3,2,1,0:T(8,128)(2,1)S(1)}, bf16[2,2,2,2,32,2048]{5,4,3,2,1,0:T(8,128)(2,1)}, u32[]{:S(2)}) copy-start(bf16[2,2,2,2,32,2048]{5,4,3,2,1,0:T(8,128)(2,1)} %get-tuple-element.9) | copy-start | bytes 6291460
  56.2 1.6 copy-start.4
  62.1 27.2 %all-to-all-start.1 = ((bf16[16,64,512]{2,1,0:T(8,128)(2,1)}), bf16[16,64,512]{2,1,0:T(8,128)(2,1)}, u32[]{:S(2)}, u32[]{:S(2)}) async-start(bf16[16,64,512]{2,1,0:T(8,128)(2,1)} %fusion.17), calls=%async_computation.2 | async-start | bytes 2097152 | tf_op jit(solution)/shard_map/all_to_all | solution.py:186
  66.4 55.5 %reduce-scatter.2.cloned.1.call-start = ((), (), s32[]{:S(2)}) async-start(), calls=%async_computation.4 | async-start | bytes 3145728 | tf_op jit(solution)/shard_map/reduce_scatter | solution.py:192
  72.0 0.7 copy-start.7
  92.3 29.6 %all-to-all-start.2 = ((bf16[16,64,512]{2,1,0:T(8,128)(2,1)}), bf16[16,64,512]{2,1,0:T(8,128)(2,1)S(1)}, u32[]{:S(2)}, u32[]{:S(2)}) async-start(bf16[16,64,512]{2,1,0:T(8,128)(2,1)} %broadcast_select_fusion), calls=%async_computation.3 | async-start | bytes 2097152 | tf_op jit(solution)/shard_map/all_to_all | solution.py:188
  121.9 1.0 copy-start.1
  122.9 29.7 %all-to-all-start = ((bf16[16,32,1024]{2,1,0:T(8,128)(2,1)}), bf16[16,32,1024]{2,1,0:T(8,128)(2,1)S(1)}, u32[]{:S(2)}, u32[]{:S(2)}) async-start(bf16[16,32,1024]{2,1,0:T(8,128)(2,1)} %bitcast.49), calls=%async_computation.1 | async-start | bytes 2097152 | tf_op jit(solution)/shard_map/all_to_all | solution.py:194
  131.8 1.6 copy-start.6
  136.8 3.3 %copy-start.2 = (bf16[2,2,2,2,32,2048]{5,4,3,2,1,0:T(8,128)(2,1)S(1)}, bf16[2,2,2,2,32,2048]{5,4,3,2,1,0:T(8,128)(2,1)}, u32[]{:S(2)}) copy-start(bf16[2,2,2,2,32,2048]{5,4,3,2,1,0:T(8,128)(2,1)} %get-tuple-element.12) | copy-start | bytes 6291460
Sparse Core Ops, SparseCore 0:
  72.1 33.0 reduce-scatter.1

commit v3 on v2

--- a/solution.py
+++ b/solution.py
@@ -129,6 +129,228 @@
     )
 
 
+def reduce_orders(expert_bits, dp_bits):
+    far = [("expert", b) for b in range(2, expert_bits)]
+    mid = [("expert", 1)]
+    near = [("expert", 0)]
+    across = [("dp", b) for b in range(dp_bits - 1, -1, -1)]
+    return (near + across + mid + far, near + mid + across + far)
+
+
+def reduce_shapes(order, expert_bits, dp_bits, rows, width):
+    left_e, left_d = expert_bits, dp_bits
+    shapes = []
+    for axis, _ in order:
+        if axis == "expert":
+            left_e -= 1
+        else:
+            left_d -= 1
+        shapes.append((2,) * left_e + (rows, width * 2**left_d))
+    return shapes
+
+
+def exchange_kernel(n_expert, n_dp, chunks, match, packed, part, landed, result, *scratch):
+    e = lax.axis_index("expert")
+    d = lax.axis_index("dp")
+    expert_bits, dp_bits = bit_count(n_expert), bit_count(n_dp)
+    steps = expert_bits + dp_bits
+    halves = 2
+    sums = [scratch[i * steps : (i + 1) * steps] for i in range(halves)]
+    came = [scratch[(halves + i) * steps : (halves + i + 1) * steps] for i in range(halves)]
+    rest = scratch[2 * halves * steps :]
+    arrived = rest[:chunks]
+    ordered, send1, recv1, send2, recv2, own, rsend, rrecv = rest[chunks:]
+    size = packed.shape[1] // chunks
+    width = result.shape[1]
+    half = result.shape[0] // halves
+
+    def peer(axis, bit):
+        if axis == "expert":
+            return (d, flipped(e, bit))
+        return (flipped(d, bit), e)
+
+    barrier = pltpu.get_barrier_semaphore()
+
+    @pl.loop(1, n_expert)
+    def _(o):
+        pl.semaphore_signal(barrier, inc=1, device_id=(d, (e + o) % n_expert), device_id_type=MESH)
+
+    for b in range(dp_bits):
+        pl.semaphore_signal(barrier, inc=1, device_id=(flipped(d, b), e), device_id_type=MESH)
+
+    def rows_of(c):
+        return pl.ds(c * size, size)
+
+    stay = [
+        pltpu.make_async_copy(packed.at[e, rows_of(c)], arrived[c].at[e], own.at[0, c])
+        for c in range(chunks)
+    ]
+    for c in stay:
+        c.start()
+    pl.semaphore_wait(barrier, n_expert - 1 + dp_bits)
+
+    def first(c, o):
+        to = (e + o) % n_expert
+        return pltpu.make_async_remote_copy(
+            src_ref=packed.at[to, rows_of(c)],
+            dst_ref=arrived[c].at[e],
+            send_sem=send1.at[c, o],
+            recv_sem=recv1.at[c, o],
+            device_id=(d, to),
+            device_id_type=MESH,
+        )
+
+    def second(c, o):
+        return pltpu.make_async_remote_copy(
+            src_ref=ordered.at[o, rows_of(c)],
+            dst_ref=landed.at[e, rows_of(c)],
+            send_sem=send2.at[c, o],
+            recv_sem=recv2.at[c, o],
+            device_id=(d, (e + o) % n_expert),
+            device_id_type=MESH,
+        )
+
+    orders = reduce_orders(expert_bits, dp_bits)
+    flights = [[], []]
+
+    def split(i, s):
+        axis, bit = orders[i][s]
+        if s == 0:
+            ref, rows = part, pl.ds(i * half, half)
+        else:
+            ref, rows = sums[i][s - 1], slice(None)
+        left = [b for a, b in orders[i][s:] if a == "expert"]
+        left = sorted(left, reverse=True)
+        if axis == "expert":
+            mine = (e // 2**bit) % 2
+            at = left.index(bit)
+
+            def where(v):
+                return tuple([slice(None)] * at + [v] + [slice(None)] * (len(left) - at - 1)) + (
+                    rows,
+                    slice(None),
+                )
+
+            return ref, where(mine), where(1 - mine)
+        mine = (d // 2**bit) % 2
+        span = 2**bit * width
+        head = (slice(None),) * len(left) + (rows,)
+        keep = head + (pl.ds(pl.multiple_of(mine * span, 128), span),)
+        give = head + (pl.ds(pl.multiple_of((1 - mine) * span, 128), span),)
+        return ref, keep, give
+
+    def start_step(i, s):
+        ref, _, give = split(i, s)
+        c = pltpu.make_async_remote_copy(
+            src_ref=ref.at[give],
+            dst_ref=came[i][s],
+            send_sem=rsend.at[i, s],
+            recv_sem=rrecv.at[i, s],
+            device_id=peer(*orders[i][s]),
+            device_id_type=MESH,
+        )
+        c.start()
+        flights[i].append(c)
+
+    def end_step(i, s):
+        ref, keep, _ = split(i, s)
+        flights[i][s].wait_recv()
+        total = ref[keep].astype(jnp.float32) + came[i][s][...].astype(jnp.float32)
+        sums[i][s][...] = total.astype(sums[i][s].dtype)
+
+    for i in range(halves):
+        start_step(i, 0)
+    for c in range(chunks):
+
+        @pl.loop(1, n_expert)
+        def _(o):
+            first(c, o).start()
+
+    early = min(2, steps - 1)
+    for s in range(early):
+        for i in range(halves):
+            end_step(i, s)
+            start_step(i, s + 1)
+    for c in range(chunks):
+        stay[c].wait()
+
+        @pl.loop(1, n_expert)
+        def _(o):
+            first(c, o).wait_recv()
+
+        @pl.loop(0, n_expert)
+        def _(o):
+            source = match[(e + o) % n_expert]
+            ordered[o, rows_of(c), :] = arrived[c][source]
+
+        pltpu.make_async_copy(
+            ordered.at[0, rows_of(c)], landed.at[e, rows_of(c)], own.at[1, c]
+        ).start()
+
+        @pl.loop(1, n_expert)
+        def _(o):
+            second(c, o).start()
+
+    for s in range(early, steps):
+        for i in range(halves):
+            end_step(i, s)
+            if s + 1 < steps:
+                start_step(i, s + 1)
+    for i in range(halves):
+        result[pl.ds(i * half, half), :] = sums[i][steps - 1][...]
+    for c in range(chunks):
+        pltpu.make_async_copy(
+            ordered.at[0, rows_of(c)], landed.at[e, rows_of(c)], own.at[1, c]
+        ).wait()
+
+        @pl.loop(1, n_expert)
+        def _(o):
+            second(c, o).wait_recv()
+            first(c, o).wait_send()
+            second(c, o).wait_send()
+
+    for f in flights:
+        for c in f:
+            c.wait_send()
+
+
+def exchange(n_expert, n_dp, matching, packed, part, tok_rows, width):
+    expert_bits, dp_bits = bit_count(n_expert), bit_count(n_dp)
+    steps = expert_bits + dp_bits
+    chunks = 2 if packed.shape[1] % 32 == 0 else 1
+    buffers = []
+    for order in reduce_orders(expert_bits, dp_bits):
+        for shape in reduce_shapes(order, expert_bits, dp_bits, tok_rows // 2, width):
+            buffers.append(pltpu.VMEM(shape, part.dtype))
+    return pl.pallas_call(
+        functools.partial(exchange_kernel, n_expert, n_dp, chunks),
+        out_shape=(
+            jax.ShapeDtypeStruct(packed.shape, packed.dtype),
+            jax.ShapeDtypeStruct((tok_rows, width), part.dtype),
+        ),
+        in_specs=[
+            pl.BlockSpec(memory_space=pltpu.SMEM),
+            pl.BlockSpec(memory_space=pltpu.VMEM),
+            pl.BlockSpec(memory_space=pltpu.VMEM),
+        ],
+        out_specs=[pl.BlockSpec(memory_space=pltpu.VMEM)] * 2,
+        scratch_shapes=buffers
+        + buffers
+        + [pltpu.VMEM((n_expert, packed.shape[1] // chunks, packed.shape[2]), packed.dtype)] * chunks
+        + [
+            pltpu.VMEM(packed.shape, packed.dtype),
+            pltpu.SemaphoreType.DMA((chunks, n_expert)),
+            pltpu.SemaphoreType.DMA((chunks, n_expert)),
+            pltpu.SemaphoreType.DMA((chunks, n_expert)),
+            pltpu.SemaphoreType.DMA((chunks, n_expert)),
+            pltpu.SemaphoreType.DMA((2, chunks)),
+            pltpu.SemaphoreType.DMA((2, steps)),
+            pltpu.SemaphoreType.DMA((2, steps)),
+        ],
+        compiler_params=pltpu.CompilerParams(collective_id=1, has_side_effects=True),
+    )(matching, packed, part.reshape((2,) * expert_bits + (tok_rows, part.shape[1])))
+
+
 def column(table, index):
     lanes = lax.broadcasted_iota(jnp.int32, table.shape, 1)
     return jnp.sum(jnp.where(lanes == index, table, 0.0), axis=1)
@@ -183,16 +405,12 @@
     packed = jnp.einsum(
         "jrt,jth->jrh", pick, stacked, preferred_element_type=jnp.float32
     ).astype(jnp.bfloat16)
-    spread = lax.all_to_all(packed, "expert", split_axis=0, concat_axis=0, tiled=True)
-    ordered = jnp.take(spread, matching, axis=0)
-    landed = lax.all_to_all(ordered, "expert", split_axis=0, concat_axis=0, tiled=True)
     part = lax.dot_general(gate_back, w_gate, contract_cols, preferred_element_type=jnp.float32)
     part = part + lax.dot_general(up_back, w_up, contract_cols, preferred_element_type=jnp.float32)
     part = part.astype(jnp.bfloat16)
-    summed = lax.psum_scatter(part, "dp", scatter_dimension=1, tiled=True)
-    summed = summed.reshape(experts, tok_rows, summed.shape[1])
-    back = lax.all_to_all(summed, "expert", split_axis=0, concat_axis=0, tiled=True)
-    input_grad = jnp.sum(back.astype(jnp.float32), axis=0).astype(jnp.bfloat16)
+    landed, input_grad = exchange(
+        n_expert, n_dp, matching, packed, part, tok_rows, tokens.shape[1]
+    )
     p_weight = column(table, matching[me])
     p_pick = selector(p_weight, experts, capacity, 3, slots)
     dense = jnp.einsum(

time: 162 us -> 133 us (0.82)
  Pallas kernels: 39.3 us -> 97.2 us
  waiting for transfers between devices: 48.7 us -> 0 us
  starting transfers between devices: 17.9 us -> 0 us
  between operations: 14.2 us -> 0.78 us
  other arithmetic: 8.67 us -> 4.96 us
  local copies, waits for them, and re-layouts: 8.31 us -> 5.8 us
    pallas_call x0 -> x1, Pallas kernels: none -> 57.8 us  [exchange(): pl.pallas_call(functools.partial(exchange_kernel, n_expert, n_dp, chunks)...]
    all_to_all x3 -> x0, waiting for transfers between devices: 48.7 us -> none  [the longest x1 22.9 us: local(): lax.all_to_all(ordered, 'expert', split_axis=0, concat_axis=0, tiled=True)]
    all_to_all x3 -> x0, starting transfers between devices: 17.9 us -> none  [the longest x1 6.8 us: local(): lax.all_to_all(summed, 'expert', split_axis=0, concat_axis=0, tiled=True)]
    dot_general x1, matrix products: 1.64 us -> 3.62 us  [local(): upper = jnp.dot(rows, w_up, preferred_element_type=jnp.float32)]
    gather x1 -> x0, local copies, waits for them, and re-layouts: 1.84 us -> none  [local(): ordered = jnp.take(spread, matching, axis=0)]
    convert_element_type x1, other arithmetic: 3.78 us -> 2.04 us  [scaled(): (cotangent.astype(jnp.float32) * weight[:, None]).astype(jnp.bfloat16)]
    unnamed x18 -> x19, local copies, waits for them, and re-layouts: 5.03 us -> 4.21 us
  transfers between devices with their start and end apart: 4 -> 0, of which waited for: 3 -> 0; matrix products, arithmetic and copies ran while one was open for 13% -> 0% of each run, Pallas kernels for 0% -> 0%
where the time goes in v3:
time: 133 us
  Pallas kernels  97.2 us (73%)
  matrix products  24 us (18%)
  local copies, waits for them, and re-layouts  5.8 us (4%)
  other arithmetic  4.96 us (4%)
    pallas_call x1, Pallas kernels, exchange(): pl.pallas_call(functools.partial(exchange_kernel, n_expert, n_dp, chunks)...  57.8 us
    pallas_call x1, Pallas kernels, gather_all(): pl.pallas_call(functools.partial(gather_kernel, n_expert, n_dp), out_shap...  39.3 us
    unnamed x19, local copies, waits for them, and re-layouts  4.21 us
    dot_general x1, matrix products, local(): upper = jnp.dot(rows, w_up, preferred_element_type=jnp.float32)  3.62 us
    dot_general x1, matrix products, local(): lax.dot_general(rows, take(0), contract_rows, preferred_element_type=jnp....  3.32 us
    dot_general x1, matrix products, local(): lax.dot_general(rows, take(1), contract_rows, preferred_element_type=jnp....  3.32 us
    dot_general x1, matrix products, local(): lax.dot_general(p_grads, take(2), contract_rows, preferred_element_type=j...  3.32 us

profile of v3, /device:TPU:0, one launch (start us, length us, event | category | flops | bytes accessed | tf_op | source)
XLA Modules:
  0.0 132.7 jit_solution(14985421734303323868)
XLA Ops:
  0.6 1.4 %dynamic_slice.3 = s32[1]{0:T(128)} dynamic-slice(s32[16]{0:T(128)} %match.1, s32[]{:T(128)S(6)} %select_n.51), dynamic_slice_sizes={1} | dynamic-slice | bytes 12 | tf_op jit(solution)/shard_map/dynamic_slice | solution.py:414
  2.0 0.6 iota_compare_fusion.4
  2.7 0.8 copy.14
  3.5 0.8 copy.15
  4.3 0.7 select_reduce_fusion.2.table
  5.0 39.3 %shard_map.111 = (bf16[2,2,2,2,32,2048]{5,4,3,2,1,0:T(8,128)(2,1)}, bf16[2,2,2,2,32,2048]{5,4,3,2,1,0:T(8,128)(2,1)}, f32[2,2,2,2,32,128]{5,4,3,2,1,0:T(8,128)}) custom-call(bf16[32,1024]{1,0:T(8,128)(2,1)} %tokens.1, bf16[32,1024]{1,0:T(8,128)(2,1)} %cotangent.1, f32[32,128]{1,0:T(8,128)} %select_reduce_fusion.2.table), custom_call_target="tpu_custom_call" | custom-call | tf_op jit(solution)/shard_map/pallas_call | solution.py:112
  44.3 1.2 select_reduce_fusion
  46.1 3.6 %fusion.7 = f32[512,512]{1,0:T(8,128)S(1)} fusion(bf16[512,2048]{1,0:T(8,128)(2,1)} %bitcast.54, bf16[1,2048,512]{2,1,0:T(8,128)(2,1)} %param.14), kind=kOutput, calls=%fused_computation.13 | convolution fusion | flops 1073741824 | bytes 5242880 | tf_op jit(solution)/shard_map/dot_general | solution.py:396
  49.8 2.0 %fusion.1 = (bf16[2,2,2,2,32,2048]{5,4,3,2,1,0:T(8,128)(2,1)}, bf16[2,2,2,2,32,2048]{5,4,3,2,1,0:T(8,128)(2,1)S(1)}) fusion(bf16[2,2,2,2,32,2048]{5,4,3,2,1,0:T(8,128)(2,1)S(1)} %copy-done.3, f32[2,2,2,2,32]{4,3,2,1,0:T(2,128)S(1)} %get-tuple-element.14, f32[2,2,2,2,32]{4,3,2,1,0:T(2,128)S(1)} %get-tuple-element.15), kind=kLoop, calls=%fused_computation.3 | loop fusion | flops 5242880 | bytes 6295552 | tf_op jit(solution)/shard_map/convert_element_type | solution.py:360
  51.8 1.2 fusion.9
  53.1 0.3 copy-done.6
  53.4 1.7 %multiply_convert_fusion.2 = (bf16[512,512]{1,0:T(8,128)(2,1)S(1)}, bf16[512,512]{1,0:T(8,128)(2,1)S(1)}, bf16[512,512]{1,0:T(8,128)(2,1)S(1)}) fusion(f32[512,512]{1,0:T(8,128)S(1)} %fusion.9, f32[512,512]{1,0:T(8,128)S(1)} %fusion.7, bf16[512,2048]{1,0:T(8,128)(2,1)S(1)} %bitcast.55, bf16[1,2048,512]{2,1,0:T(8,128)(2,1)S(1)} %copy-done), kind=kOutput, calls=%fused_computation.33 | convolution fusion | flops 1077936128 | bytes 7864320 | tf_op jit(solution)/shard_map/dot_general | solution.py:395
  55.2 1.4 %fusion.17.packed = bf16[16,64,512]{2,1,0:T(8,128)(2,1)} fusion(bf16[16,32,512]{2,1,0:T(8,128)(2,1)S(1)} %bitcast.58, bf16[16,32,512]{2,1,0:T(8,128)(2,1)S(1)} %bitcast.50, bf16[16,32,512]{2,1,0:T(8,128)(2,1)S(1)} %bitcast.49, s32[96]{0:T(128)S(1)} %get-tuple-element.26, s32[96]{0:T(128)S(1)} %get-tuple-element.27, s32[16,96]{1,0:T(8,128)S(1)} %pad_add_fusion, ...), kind=kOutput, calls=%fused_computation.24 | convolution fusion | flops 106594304 | bytes 2629984 | tf_op jit(solution)/shard_map/jrt,jth->jrh/dot_general | solution.py:405
  56.6 1.3 fusion.2
  57.9 0.3 copy-done.1
  58.2 2.6 %add_convert_fusion = bf16[512,2048]{1,0:T(8,128)(2,1)} fusion(f32[512,2048]{1,0:T(8,128)S(1)} %fusion.2, bf16[512,512]{1,0:T(8,128)(2,1)S(1)} %get-tuple-element.19, bf16[1,2048,512]{2,1,0:T(8,128)(2,1)S(1)} %copy-done.1), kind=kOutput, calls=%fused_computation.4 | convolution fusion | flops 1075838976 | bytes 8912896 | tf_op jit(solution)/shard_map/dot_general | solution.py:409
  60.8 57.8 %shard_map.112 = (bf16[16,64,512]{2,1,0:T(8,128)(2,1)}, bf16[32,1024]{1,0:T(8,128)(2,1)}) custom-call(s32[16]{0:T(128)} %match.1, bf16[16,64,512]{2,1,0:T(8,128)(2,1)} %fusion.17.packed, bf16[2,2,2,2,32,2048]{5,4,3,2,1,0:T(8,128)(2,1)} %bitcast.46), custom_call_target="tpu_custom_call" | custom-call | tf_op jit(solution)/shard_map/pallas_call | solution.py:325
  118.6 1.9 %convolution_convert_fusion = bf16[16,96,512]{2,1,0:T(8,128)(2,1)S(1)} fusion(bf16[16,64,512]{2,1,0:T(8,128)(2,1)} %get-tuple-element.13, s32[16,96]{1,0:T(8,128)S(1)} %pad_add_fusion.1, s32[96]{0:T(128)S(1)} %get-tuple-element.26, s32[96]{0:T(128)S(1)} %get-tuple-element.27, pred[16,96]{1,0:T(8,128)(4,1)S(1)} %broadcast_compare_fusion, ...), kind=kOutput, calls=%fused_computation.17 | convolution fusion | flops 102137856 | bytes 2629984 | tf_op jit(solution)/shard_map/jrt,jrh->jth/dot_general | solution.py:416
  120.5 0.2 fusion.57
  120.7 1.4 %copy-done.2 = bf16[2,2,2,2,32,2048]{5,4,3,2,1,0:T(8,128)(2,1)S(1)} copy-done((bf16[2,2,2,2,32,2048]{5,4,3,2,1,0:T(8,128)(2,1)S(1)}, bf16[2,2,2,2,32,2048]{5,4,3,2,1,0:T(8,128)(2,1)}, u32[]{:S(2)}) %copy-start.2) | copy-done | bytes 2097176
  122.1 3.3 %convolution_bitcast_fusion = f32[1,2048,512]{2,1,0:T(8,128)} fusion(bf16[512,2048]{1,0:T(8,128)(2,1)S(1)} %bitcast.47, bf16[512,512]{1,0:T(8,128)(2,1)S(1)} %bitcast.53), kind=kOutput, calls=%fused_computation.5 | convolution fusion | flops 1073741824 | bytes 6815744 | tf_op jit(solution)/shard_map/dot_general | solution.py:427
  125.4 3.3 %convolution_bitcast_fusion.1 = f32[1,2048,512]{2,1,0:T(8,128)} fusion(bf16[512,2048]{1,0:T(8,128)(2,1)S(1)} %bitcast.56, bf16[512,512]{1,0:T(8,128)(2,1)S(1)} %bitcast.52), kind=kOutput, calls=%fused_computation.6 | convolution fusion | flops 1073741824 | bytes 6815744 | tf_op jit(solution)/shard_map/dot_general | solution.py:426
  128.7 3.3 %convolution_bitcast_fusion.2 = f32[1,2048,512]{2,1,0:T(8,128)} fusion(bf16[512,2048]{1,0:T(8,128)(2,1)S(1)} %bitcast.57, bf16[512,512]{1,0:T(8,128)(2,1)S(1)} %bitcast.51), kind=kOutput, calls=%fused_computation.7 | convolution fusion | flops 1073741824 | bytes 6815744 | tf_op jit(solution)/shard_map/dot_general | solution.py:425
  132.1 0.6 copy.17
  (25 shorter events, 0.7 us)
Async XLA Ops:
  0.6 52.5 %copy-start = (bf16[1,2048,512]{2,1,0:T(8,128)(2,1)S(1)}, bf16[1,2048,512]{2,1,0:T(8,128)(2,1)}, u32[]{:S(2)}) copy-start(bf16[1,2048,512]{2,1,0:T(8,128)(2,1)} %param.13) | copy-start | bytes 6291460
  46.1 3.6 %copy-start.3 = (bf16[2,2,2,2,32,2048]{5,4,3,2,1,0:T(8,128)(2,1)S(1)}, bf16[2,2,2,2,32,2048]{5,4,3,2,1,0:T(8,128)(2,1)}, u32[]{:S(2)}) copy-start(bf16[2,2,2,2,32,2048]{5,4,3,2,1,0:T(8,128)(2,1)} %get-tuple-element.10) | copy-start | bytes 6291460
  49.8 2.1 %copy-start.5 = (bf16[1,2048,512]{2,1,0:T(8,128)(2,1)S(1)}, bf16[1,2048,512]{2,1,0:T(8,128)(2,1)}, u32[]{:S(2)}) copy-start(bf16[1,2048,512]{2,1,0:T(8,128)(2,1)} %param.15) | copy-start | bytes 6291460
  51.8 1.6 %copy-start.6 = (bf16[2,2,2,2,32,2048]{5,4,3,2,1,0:T(8,128)(2,1)S(1)}, bf16[2,2,2,2,32,2048]{5,4,3,2,1,0:T(8,128)(2,1)}, u32[]{:S(2)}) copy-start(bf16[2,2,2,2,32,2048]{5,4,3,2,1,0:T(8,128)(2,1)} %get-tuple-element.11) | copy-start | bytes 6291460
  56.6 1.6 %copy-start.1 = (bf16[1,2048,512]{2,1,0:T(8,128)(2,1)S(1)}, bf16[1,2048,512]{2,1,0:T(8,128)(2,1)}, u32[]{:S(2)}) copy-start(bf16[1,2048,512]{2,1,0:T(8,128)(2,1)} %param.14) | copy-start | bytes 6291460
  120.5 1.6 %copy-start.2 = (bf16[2,2,2,2,32,2048]{5,4,3,2,1,0:T(8,128)(2,1)S(1)}, bf16[2,2,2,2,32,2048]{5,4,3,2,1,0:T(8,128)(2,1)}, u32[]{:S(2)}) copy-start(bf16[2,2,2,2,32,2048]{5,4,3,2,1,0:T(8,128)(2,1)} %get-tuple-element.16) | copy-start | bytes 6291460
  122.1 3.3 %copy-start.7 = (bf16[2,2,2,2,32,2048]{5,4,3,2,1,0:T(8,128)(2,1)S(1)}, bf16[2,2,2,2,32,2048]{5,4,3,2,1,0:T(8,128)(2,1)}, u32[]{:S(2)}) copy-start(bf16[2,2,2,2,32,2048]{5,4,3,2,1,0:T(8,128)(2,1)} %get-tuple-element.11) | copy-start | bytes 6291460
  128.7 3.3 %copy-start.4 = (bf16[32,1024]{1,0:T(8,128)(2,1)S(1)}, bf16[32,1024]{1,0:T(8,128)(2,1)}, u32[]{:S(2)}) copy-start(bf16[32,1024]{1,0:T(8,128)(2,1)} %get-tuple-element.32) | copy-start | bytes 196612

commit v4 on v3

--- a/solution.py
+++ b/solution.py
@@ -26,7 +26,13 @@
     mid = [("expert", 1)]
     last = [("expert", 0)]
     across = [("dp", b) for b in range(dp_bits)]
-    return (far + across + mid + last, far + mid + across + last, far + mid + last)
+    return (
+        far + across + mid + last,
+        far + mid + across + last,
+        across + far + mid + last,
+        mid + far + across + last,
+        far + mid + last,
+    )
 
 
 def gather_kernel(
@@ -61,14 +67,14 @@
     for link in links:
         pl.semaphore_signal(barrier, inc=1, device_id=peer(*link), device_id_type=MESH)
 
-    first, second, plain = gather_orders(expert_bits, dp_bits)
+    orders = gather_orders(expert_bits, dp_bits)
     top, low, whole = pl.ds(0, half), pl.ds(half, half), pl.ds(0, 2 * half)
     parts = [
-        (tokens, all_tokens, top, first, True),
-        (tokens, all_tokens, low, second, True),
-        (cotangent, all_cotangent, top, first, True),
-        (cotangent, all_cotangent, low, second, True),
-        (table, all_table, whole, plain, False),
+        (tokens, all_tokens, top, orders[0], True),
+        (tokens, all_tokens, low, orders[2], True),
+        (cotangent, all_cotangent, top, orders[1], True),
+        (cotangent, all_cotangent, low, orders[3], True),
+        (table, all_table, whole, orders[4], False),
     ]
     locals_ = []
     for i, (src, dst, rows, order, data) in enumerate(parts):
@@ -79,7 +85,9 @@
     flights = [[] for _ in parts]
     steps = max(len(p[3]) for p in parts)
     for s in range(steps):
-        for i, (src, dst, rows, order, data) in enumerate(parts):
+        turn = (4, 1, 3, 0, 2) if s < 2 else (4, 0, 2, 1, 3)
+        for i in turn:
+            src, dst, rows, order, data = parts[i]
             if s >= len(order):
                 continue
             if s == 0:
@@ -411,7 +419,8 @@
     landed, input_grad = exchange(
         n_expert, n_dp, matching, packed, part, tok_rows, tokens.shape[1]
     )
-    p_weight = column(table, matching[me])
+    partner = jnp.sum(jnp.where(jnp.arange(experts) == me, matching, 0))
+    p_weight = column(table, partner)
     p_pick = selector(p_weight, experts, capacity, 3, slots)
     dense = jnp.einsum(
         "jrt,jrh->jth", p_pick, landed, preferred_element_type=jnp.float32

time: 133 us -> 131 us (0.985)
  Pallas kernels: 97.2 us -> 94.5 us
  other arithmetic: 4.96 us -> 6.4 us
  local copies, waits for them, and re-layouts: 5.8 us -> 4.41 us
    reduce_sum x0 -> x1, other arithmetic: none -> 1.44 us  [local(): partner = jnp.sum(jnp.where(jnp.arange(experts) == me, matching, 0))]
    dynamic_slice x1 -> x0, local copies, waits for them, and re-layouts: 1.39 us -> none  [local(): p_weight = column(table, matching[me])]
    pallas_call x1, Pallas kernels: 57.8 us -> 56.5 us  [exchange(): pl.pallas_call(functools.partial(exchange_kernel, n_expert, n_dp, chunks)...]
where the time goes in v4:
time: 131 us; the launch traced here: 130 us
  Pallas kernels  94.5 us (72%)
  matrix products  24 us (18%)
  other arithmetic  6.4 us (5%)
  local copies, waits for them, and re-layouts  4.41 us (3%)
    pallas_call x1, Pallas kernels, exchange(): pl.pallas_call(functools.partial(exchange_kernel, n_expert, n_dp, chunks)...  56.5 us
    pallas_call x1, Pallas kernels, gather_all(): pl.pallas_call(functools.partial(gather_kernel, n_expert, n_dp), out_shap...  38 us
    unnamed x19, local copies, waits for them, and re-layouts  4.21 us
    dot_general x1, matrix products, local(): upper = jnp.dot(rows, w_up, preferred_element_type=jnp.float32)  3.62 us
    dot_general x1, matrix products, local(): lax.dot_general(rows, take(0), contract_rows, preferred_element_type=jnp....  3.32 us
    dot_general x1, matrix products, local(): lax.dot_general(rows, take(1), contract_rows, preferred_element_type=jnp....  3.32 us
    dot_general x1, matrix products, local(): lax.dot_general(p_grads, take(2), contract_rows, preferred_element_type=j...  3.32 us

profile of v4, /device:TPU:0, one launch (start us, length us, event | category | flops | bytes accessed | tf_op | source)
XLA Modules:
  0.0 130.1 jit_solution(10117214430543814286)
XLA Ops:
  0.6 1.4 %fusion.46 = s32[]{:T(128)} fusion(s32[16]{0:T(128)} %match.1, s32[]{:T(128)S(6)} %axis_index.12), kind=kLoop, calls=%fused_computation.79 | loop fusion | flops 47 | bytes 72 | tf_op jit(solution)/shard_map/reduce_sum | solution.py:422
  2.1 0.6 iota_compare_fusion.4
  2.8 0.8 copy.14
  3.5 0.8 copy.15
  4.3 0.7 select_reduce_fusion.2.table
  5.1 38.0 %shard_map.111 = (bf16[2,2,2,2,32,2048]{5,4,3,2,1,0:T(8,128)(2,1)}, bf16[2,2,2,2,32,2048]{5,4,3,2,1,0:T(8,128)(2,1)}, f32[2,2,2,2,32,128]{5,4,3,2,1,0:T(8,128)}) custom-call(bf16[32,1024]{1,0:T(8,128)(2,1)} %tokens.1, bf16[32,1024]{1,0:T(8,128)(2,1)} %cotangent.1, f32[32,128]{1,0:T(8,128)} %select_reduce_fusion.2.table), custom_call_target="tpu_custom_call" | custom-call | tf_op jit(solution)/shard_map/pallas_call | solution.py:120
  43.1 1.2 select_reduce_fusion
  44.9 3.6 %fusion.7 = f32[512,512]{1,0:T(8,128)S(1)} fusion(bf16[512,2048]{1,0:T(8,128)(2,1)} %bitcast.53, bf16[1,2048,512]{2,1,0:T(8,128)(2,1)} %param.14), kind=kOutput, calls=%fused_computation.13 | convolution fusion | flops 1073741824 | bytes 5242880 | tf_op jit(solution)/shard_map/dot_general | solution.py:404
  48.6 2.0 %fusion.1 = (bf16[2,2,2,2,32,2048]{5,4,3,2,1,0:T(8,128)(2,1)}, bf16[2,2,2,2,32,2048]{5,4,3,2,1,0:T(8,128)(2,1)S(1)}) fusion(bf16[2,2,2,2,32,2048]{5,4,3,2,1,0:T(8,128)(2,1)S(1)} %copy-done.3, f32[2,2,2,2,32]{4,3,2,1,0:T(2,128)S(1)} %get-tuple-element.14, f32[2,2,2,2,32]{4,3,2,1,0:T(2,128)S(1)} %get-tuple-element.15), kind=kLoop, calls=%fused_computation.3 | loop fusion | flops 5242880 | bytes 6295552 | tf_op jit(solution)/shard_map/convert_element_type | solution.py:368
  50.6 1.2 fusion.9
  51.9 0.3 copy-done.6
  52.2 1.7 %multiply_convert_fusion.2 = (bf16[512,512]{1,0:T(8,128)(2,1)S(1)}, bf16[512,512]{1,0:T(8,128)(2,1)S(1)}, bf16[512,512]{1,0:T(8,128)(2,1)S(1)}) fusion(f32[512,512]{1,0:T(8,128)S(1)} %fusion.9, f32[512,512]{1,0:T(8,128)S(1)} %fusion.7, bf16[512,2048]{1,0:T(8,128)(2,1)S(1)} %bitcast.54, bf16[1,2048,512]{2,1,0:T(8,128)(2,1)S(1)} %copy-done), kind=kOutput, calls=%fused_computation.33 | convolution fusion | flops 1077936128 | bytes 7864320 | tf_op jit(solution)/shard_map/dot_general | solution.py:403
  53.9 1.4 %fusion.17.packed = bf16[16,64,512]{2,1,0:T(8,128)(2,1)} fusion(bf16[16,32,512]{2,1,0:T(8,128)(2,1)S(1)} %bitcast.57, bf16[16,32,512]{2,1,0:T(8,128)(2,1)S(1)} %bitcast.49, bf16[16,32,512]{2,1,0:T(8,128)(2,1)S(1)} %bitcast.48, s32[96]{0:T(128)S(1)} %get-tuple-element.26, s32[96]{0:T(128)S(1)} %get-tuple-element.27, s32[16,96]{1,0:T(8,128)S(1)} %pad_add_fusion, ...), kind=kOutput, calls=%fused_computation.24 | convolution fusion | flops 106594304 | bytes 2629984 | tf_op jit(solution)/shard_map/jrt,jth->jrh/dot_general | solution.py:413
  55.4 1.3 %fusion.2 = f32[512,2048]{1,0:T(8,128)S(1)} fusion(bf16[512,512]{1,0:T(8,128)(2,1)S(1)} %get-tuple-element.18, bf16[1,2048,512]{2,1,0:T(8,128)(2,1)S(1)} %copy-done), kind=kOutput, calls=%fused_computation.8 | convolution fusion | flops 1073741824 | bytes 6815744 | tf_op jit(solution)/shard_map/dot_general | solution.py:416
  56.7 0.3 copy-done.1
  56.9 2.6 %add_convert_fusion = bf16[512,2048]{1,0:T(8,128)(2,1)} fusion(f32[512,2048]{1,0:T(8,128)S(1)} %fusion.2, bf16[512,512]{1,0:T(8,128)(2,1)S(1)} %get-tuple-element.19, bf16[1,2048,512]{2,1,0:T(8,128)(2,1)S(1)} %copy-done.1), kind=kOutput, calls=%fused_computation.4 | convolution fusion | flops 1075838976 | bytes 8912896 | tf_op jit(solution)/shard_map/dot_general | solution.py:417
  59.6 56.5 %shard_map.112 = (bf16[16,64,512]{2,1,0:T(8,128)(2,1)}, bf16[32,1024]{1,0:T(8,128)(2,1)}) custom-call(s32[16]{0:T(128)} %match.1, bf16[16,64,512]{2,1,0:T(8,128)(2,1)} %fusion.17.packed, bf16[2,2,2,2,32,2048]{5,4,3,2,1,0:T(8,128)(2,1)} %bitcast.45), custom_call_target="tpu_custom_call" | custom-call | tf_op jit(solution)/shard_map/pallas_call | solution.py:333
  116.0 1.9 %convolution_convert_fusion = bf16[16,96,512]{2,1,0:T(8,128)(2,1)S(1)} fusion(bf16[16,64,512]{2,1,0:T(8,128)(2,1)} %get-tuple-element.13, s32[16,96]{1,0:T(8,128)S(1)} %pad_add_fusion.1, s32[96]{0:T(128)S(1)} %get-tuple-element.26, s32[96]{0:T(128)S(1)} %get-tuple-element.27, pred[16,96]{1,0:T(8,128)(4,1)S(1)} %broadcast_compare_fusion, ...), kind=kOutput, calls=%fused_computation.17 | convolution fusion | flops 102137856 | bytes 2629984 | tf_op jit(solution)/shard_map/jrt,jrh->jth/dot_general | solution.py:425
  117.9 0.2 fusion.58
  118.1 1.4 %copy-done.2 = bf16[2,2,2,2,32,2048]{5,4,3,2,1,0:T(8,128)(2,1)S(1)} copy-done((bf16[2,2,2,2,32,2048]{5,4,3,2,1,0:T(8,128)(2,1)S(1)}, bf16[2,2,2,2,32,2048]{5,4,3,2,1,0:T(8,128)(2,1)}, u32[]{:S(2)}) %copy-start.2) | copy-done | bytes 2097176
  119.5 3.3 %convolution_bitcast_fusion = f32[1,2048,512]{2,1,0:T(8,128)} fusion(bf16[512,2048]{1,0:T(8,128)(2,1)S(1)} %bitcast.46, bf16[512,512]{1,0:T(8,128)(2,1)S(1)} %bitcast.52), kind=kOutput, calls=%fused_computation.5 | convolution fusion | flops 1073741824 | bytes 6815744 | tf_op jit(solution)/shard_map/dot_general | solution.py:436
  122.8 3.3 %convolution_bitcast_fusion.1 = f32[1,2048,512]{2,1,0:T(8,128)} fusion(bf16[512,2048]{1,0:T(8,128)(2,1)S(1)} %bitcast.55, bf16[512,512]{1,0:T(8,128)(2,1)S(1)} %bitcast.51), kind=kOutput, calls=%fused_computation.6 | convolution fusion | flops 1073741824 | bytes 6815744 | tf_op jit(solution)/shard_map/dot_general | solution.py:435
  126.1 3.3 %convolution_bitcast_fusion.2 = f32[1,2048,512]{2,1,0:T(8,128)} fusion(bf16[512,2048]{1,0:T(8,128)(2,1)S(1)} %bitcast.56, bf16[512,512]{1,0:T(8,128)(2,1)S(1)} %bitcast.50), kind=kOutput, calls=%fused_computation.7 | convolution fusion | flops 1073741824 | bytes 6815744 | tf_op jit(solution)/shard_map/dot_general | solution.py:434
  129.5 0.6 copy.17
  (25 shorter events, 0.7 us)
Async XLA Ops:
  0.6 51.2 %copy-start = (bf16[1,2048,512]{2,1,0:T(8,128)(2,1)S(1)}, bf16[1,2048,512]{2,1,0:T(8,128)(2,1)}, u32[]{:S(2)}) copy-start(bf16[1,2048,512]{2,1,0:T(8,128)(2,1)} %param.13) | copy-start | bytes 6291460
  44.9 3.6 %copy-start.3 = (bf16[2,2,2,2,32,2048]{5,4,3,2,1,0:T(8,128)(2,1)S(1)}, bf16[2,2,2,2,32,2048]{5,4,3,2,1,0:T(8,128)(2,1)}, u32[]{:S(2)}) copy-start(bf16[2,2,2,2,32,2048]{5,4,3,2,1,0:T(8,128)(2,1)} %get-tuple-element.10) | copy-start | bytes 6291460
  48.5 2.1 %copy-start.5 = (bf16[1,2048,512]{2,1,0:T(8,128)(2,1)S(1)}, bf16[1,2048,512]{2,1,0:T(8,128)(2,1)}, u32[]{:S(2)}) copy-start(bf16[1,2048,512]{2,1,0:T(8,128)(2,1)} %param.15) | copy-start | bytes 6291460
  50.6 1.6 %copy-start.6 = (bf16[2,2,2,2,32,2048]{5,4,3,2,1,0:T(8,128)(2,1)S(1)}, bf16[2,2,2,2,32,2048]{5,4,3,2,1,0:T(8,128)(2,1)}, u32[]{:S(2)}) copy-start(bf16[2,2,2,2,32,2048]{5,4,3,2,1,0:T(8,128)(2,1)} %get-tuple-element.11) | copy-start | bytes 6291460
  55.4 1.6 %copy-start.1 = (bf16[1,2048,512]{2,1,0:T(8,128)(2,1)S(1)}, bf16[1,2048,512]{2,1,0:T(8,128)(2,1)}, u32[]{:S(2)}) copy-start(bf16[1,2048,512]{2,1,0:T(8,128)(2,1)} %param.14) | copy-start | bytes 6291460
  117.9 1.6 %copy-start.2 = (bf16[2,2,2,2,32,2048]{5,4,3,2,1,0:T(8,128)(2,1)S(1)}, bf16[2,2,2,2,32,2048]{5,4,3,2,1,0:T(8,128)(2,1)}, u32[]{:S(2)}) copy-start(bf16[2,2,2,2,32,2048]{5,4,3,2,1,0:T(8,128)(2,1)} %get-tuple-element.16) | copy-start | bytes 6291460
  119.5 3.3 %copy-start.7 = (bf16[2,2,2,2,32,2048]{5,4,3,2,1,0:T(8,128)(2,1)S(1)}, bf16[2,2,2,2,32,2048]{5,4,3,2,1,0:T(8,128)(2,1)}, u32[]{:S(2)}) copy-start(bf16[2,2,2,2,32,2048]{5,4,3,2,1,0:T(8,128)(2,1)} %get-tuple-element.11) | copy-start | bytes 6291460
  126.1 3.3 %copy-start.4 = (bf16[32,1024]{1,0:T(8,128)(2,1)S(1)}, bf16[32,1024]{1,0:T(8,128)(2,1)}, u32[]{:S(2)}) copy-start(bf16[32,1024]{1,0:T(8,128)(2,1)} %get-tuple-element.32) | copy-start | bytes 196612

commit v5 on v4

--- a/solution.py
+++ b/solution.py
@@ -157,7 +157,9 @@
     return shapes
 
 
-def exchange_kernel(n_expert, n_dp, chunks, match, packed, part, landed, result, *scratch):
+def exchange_kernel(
+    n_expert, n_dp, chunks, match, packed, g_back, u_back, w_gate, w_up, landed, result, *scratch
+):
     e = lax.axis_index("expert")
     d = lax.axis_index("dp")
     expert_bits, dp_bits = bit_count(n_expert), bit_count(n_dp)
@@ -167,7 +169,7 @@
     came = [scratch[(halves + i) * steps : (halves + i + 1) * steps] for i in range(halves)]
     rest = scratch[2 * halves * steps :]
     arrived = rest[:chunks]
-    ordered, send1, recv1, send2, recv2, own, rsend, rrecv = rest[chunks:]
+    part, ordered, send1, recv1, send2, recv2, own, rsend, rrecv = rest[chunks:]
     size = packed.shape[1] // chunks
     width = result.shape[1]
     half = result.shape[0] // halves
@@ -266,13 +268,25 @@
         total = ref[keep].astype(jnp.float32) + came[i][s][...].astype(jnp.float32)
         sums[i][s][...] = total.astype(sums[i][s].dtype)
 
-    for i in range(halves):
-        start_step(i, 0)
     for c in range(chunks):
 
         @pl.loop(1, n_expert)
         def _(o):
             first(c, o).start()
+
+    model_width = w_gate.shape[0]
+    tile = min(512, model_width)
+    for t in range(0, model_width, tile):
+        piece = lax.dot_general(
+            g_back[...], w_gate[t : t + tile], contract_cols, preferred_element_type=jnp.float32
+        )
+        piece += lax.dot_general(
+            u_back[...], w_up[t : t + tile], contract_cols, preferred_element_type=jnp.float32
+        )
+        shape = part.shape[:-1] + (tile,)
+        part[..., t : t + tile] = piece.astype(part.dtype).reshape(shape)
+    for i in range(halves):
+        start_step(i, 0)
 
     early = min(2, steps - 1)
     for s in range(early):
@@ -322,30 +336,30 @@
             c.wait_send()
 
 
-def exchange(n_expert, n_dp, matching, packed, part, tok_rows, width):
+def exchange(n_expert, n_dp, matching, packed, g_back, u_back, w_gate, w_up, tok_rows, width):
     expert_bits, dp_bits = bit_count(n_expert), bit_count(n_dp)
     steps = expert_bits + dp_bits
     chunks = 2 if packed.shape[1] % 32 == 0 else 1
     buffers = []
     for order in reduce_orders(expert_bits, dp_bits):
         for shape in reduce_shapes(order, expert_bits, dp_bits, tok_rows // 2, width):
-            buffers.append(pltpu.VMEM(shape, part.dtype))
+            buffers.append(pltpu.VMEM(shape, packed.dtype))
     return pl.pallas_call(
         functools.partial(exchange_kernel, n_expert, n_dp, chunks),
         out_shape=(
             jax.ShapeDtypeStruct(packed.shape, packed.dtype),
-            jax.ShapeDtypeStruct((tok_rows, width), part.dtype),
+            jax.ShapeDtypeStruct((tok_rows, width), packed.dtype),
         ),
         in_specs=[
             pl.BlockSpec(memory_space=pltpu.SMEM),
-            pl.BlockSpec(memory_space=pltpu.VMEM),
-            pl.BlockSpec(memory_space=pltpu.VMEM),
-        ],
+        ]
+        + [pl.BlockSpec(memory_space=pltpu.VMEM)] * 5,
         out_specs=[pl.BlockSpec(memory_space=pltpu.VMEM)] * 2,
         scratch_shapes=buffers
         + buffers
         + [pltpu.VMEM((n_expert, packed.shape[1] // chunks, packed.shape[2]), packed.dtype)] * chunks
         + [
+            pltpu.VMEM((2,) * expert_bits + (tok_rows, w_gate.shape[0]), packed.dtype),
             pltpu.VMEM(packed.shape, packed.dtype),
             pltpu.SemaphoreType.DMA((chunks, n_expert)),
             pltpu.SemaphoreType.DMA((chunks, n_expert)),
@@ -356,7 +370,7 @@
             pltpu.SemaphoreType.DMA((2, steps)),
         ],
         compiler_params=pltpu.CompilerParams(collective_id=1, has_side_effects=True),
-    )(matching, packed, part.reshape((2,) * expert_bits + (tok_rows, part.shape[1])))
+    )(matching, packed, g_back, u_back, w_gate, w_up)
 
 
 def column(table, index):
@@ -413,11 +427,8 @@
     packed = jnp.einsum(
         "jrt,jth->jrh", pick, stacked, preferred_element_type=jnp.float32
     ).astype(jnp.bfloat16)
-    part = lax.dot_general(gate_back, w_gate, contract_cols, preferred_element_type=jnp.float32)
-    part = part + lax.dot_general(up_back, w_up, contract_cols, preferred_element_type=jnp.float32)
-    part = part.astype(jnp.bfloat16)
     landed, input_grad = exchange(
-        n_expert, n_dp, matching, packed, part, tok_rows, tokens.shape[1]
+        n_expert, n_dp, matching, packed, gate_back, up_back, w_gate, w_up, tok_rows, tokens.shape[1]
     )
     partner = jnp.sum(jnp.where(jnp.arange(experts) == me, matching, 0))
     p_weight = column(table, partner)

time: 131 us -> 128 us (0.977)
  matrix products: 24 us -> 20 us
    dot_general x2 -> x0, matrix products: 3.91 us -> none  [the longest x1 2.61 us: local(): lax.dot_general(up_back, w_up, contract_cols, preferred_element_type=jnp....]
    unnamed x19 -> x21, local copies, waits for them, and re-layouts: 4.21 us -> 4.57 us
where the time goes in v5:
time: 128 us; the launch traced here: 127 us
  Pallas kernels  95.5 us (75%)
  matrix products  20 us (16%)
  other arithmetic  6.4 us (5%)
  local copies, waits for them, and re-layouts  4.78 us (4%)
    pallas_call x1, Pallas kernels, exchange(): pl.pallas_call(functools.partial(exchange_kernel, n_expert, n_dp, chunks)...  57.5 us
    pallas_call x1, Pallas kernels, gather_all(): pl.pallas_call(functools.partial(gather_kernel, n_expert, n_dp), out_shap...  38 us
    unnamed x21, local copies, waits for them, and re-layouts  4.57 us
    dot_general x1, matrix products, local(): upper = jnp.dot(rows, w_up, preferred_element_type=jnp.float32)  3.62 us
    dot_general x1, matrix products, local(): lax.dot_general(p_grads, take(2), contract_rows, preferred_element_type=j...  3.32 us
    dot_general x1, matrix products, local(): lax.dot_general(rows, take(1), contract_rows, preferred_element_type=jnp....  3.32 us
    dot_general x1, matrix products, local(): lax.dot_general(rows, take(0), contract_rows, preferred_element_type=jnp....  3.32 us

profile of v5, /device:TPU:0, one launch (start us, length us, event | category | flops | bytes accessed | tf_op | source)
XLA Modules:
  0.0 127.5 jit_solution(15361676700616401505)
XLA Ops:
  0.6 1.4 %fusion.39 = s32[]{:T(128)} fusion(s32[16]{0:T(128)} %match.1, s32[]{:T(128)S(6)} %axis_index.12), kind=kLoop, calls=%fused_computation.71 | loop fusion | flops 47 | bytes 72 | tf_op jit(solution)/shard_map/reduce_sum | solution.py:433
  2.1 0.6 iota_compare_fusion.4
  2.8 0.8 copy.14
  3.5 0.8 copy.15
  4.3 0.7 select_reduce_fusion.2.table
  5.1 38.0 %shard_map.111 = (bf16[2,2,2,2,32,2048]{5,4,3,2,1,0:T(8,128)(2,1)}, bf16[2,2,2,2,32,2048]{5,4,3,2,1,0:T(8,128)(2,1)}, f32[2,2,2,2,32,128]{5,4,3,2,1,0:T(8,128)}) custom-call(bf16[32,1024]{1,0:T(8,128)(2,1)} %tokens.1, bf16[32,1024]{1,0:T(8,128)(2,1)} %cotangent.1, f32[32,128]{1,0:T(8,128)} %select_reduce_fusion.2.table), custom_call_target="tpu_custom_call" | custom-call | tf_op jit(solution)/shard_map/pallas_call | solution.py:120
  43.1 1.2 select_reduce_fusion
  44.3 0.1 fusion.16
  44.6 0.1 fusion.14
  44.9 3.6 %fusion.43 = f32[512,512]{1,0:T(8,128)S(1)} fusion(bf16[512,2048]{1,0:T(8,128)(2,1)} %bitcast.47, bf16[1,2048,512]{2,1,0:T(8,128)(2,1)} %param.14), kind=kOutput, calls=%fused_computation.78 | convolution fusion | flops 1073741824 | bytes 5242880 | tf_op jit(solution)/shard_map/dot_general | solution.py:418
  48.5 2.0 %fusion.1 = (bf16[2,2,2,2,32,2048]{5,4,3,2,1,0:T(8,128)(2,1)}, bf16[2,2,2,2,32,2048]{5,4,3,2,1,0:T(8,128)(2,1)S(1)}) fusion(bf16[2,2,2,2,32,2048]{5,4,3,2,1,0:T(8,128)(2,1)S(1)} %copy-done.3, f32[2,2,2,2,32]{4,3,2,1,0:T(2,128)S(1)} %get-tuple-element.14, f32[2,2,2,2,32]{4,3,2,1,0:T(2,128)S(1)} %get-tuple-element.15), kind=kLoop, calls=%fused_computation.3 | loop fusion | flops 5242880 | bytes 6295552 | tf_op jit(solution)/shard_map/convert_element_type | solution.py:382
  50.6 1.2 fusion.2
  51.8 0.3 copy-done.1
  52.2 0.6 copy-done.7
  52.8 1.7 %multiply_convert_fusion.2 = (bf16[512,512]{1,0:T(8,128)(2,1)S(1)}, bf16[512,512]{1,0:T(8,128)(2,1)S(1)}, bf16[512,512]{1,0:T(8,128)(2,1)S(1)}) fusion(f32[512,512]{1,0:T(8,128)S(1)} %fusion.2, f32[512,512]{1,0:T(8,128)S(1)} %fusion.43, bf16[512,2048]{1,0:T(8,128)(2,1)S(1)} %bitcast.48, bf16[1,2048,512]{2,1,0:T(8,128)(2,1)S(1)} %copy-done.1), kind=kOutput, calls=%fused_computation.25 | convolution fusion | flops 1077936128 | bytes 7864320 | tf_op jit(solution)/shard_map/dot_general | solution.py:417
  54.5 1.4 %fusion.10.packed = bf16[16,64,512]{2,1,0:T(8,128)(2,1)} fusion(bf16[16,32,512]{2,1,0:T(8,128)(2,1)S(1)} %bitcast.51, bf16[16,32,512]{2,1,0:T(8,128)(2,1)S(1)} %bitcast.43, bf16[16,32,512]{2,1,0:T(8,128)(2,1)S(1)} %bitcast.42, s32[96]{0:T(128)S(1)} %get-tuple-element.26, s32[96]{0:T(128)S(1)} %get-tuple-element.27, s32[16,96]{1,0:T(8,128)S(1)} %pad_add_fusion, ...), kind=kOutput, calls=%fused_computation.16 | convolution fusion | flops 106594304 | bytes 2629984 | tf_op jit(solution)/shard_map/jrt,jth->jrh/dot_general | solution.py:427
  56.0 57.5 %shard_map.112 = (bf16[16,64,512]{2,1,0:T(8,128)(2,1)}, bf16[32,1024]{1,0:T(8,128)(2,1)}) custom-call(s32[16]{0:T(128)} %match.1, bf16[16,64,512]{2,1,0:T(8,128)(2,1)} %fusion.10.packed, bf16[512,512]{1,0:T(8,128)(2,1)} %copy-done.4, bf16[512,512]{1,0:T(8,128)(2,1)} %copy-done.5, bf16[2048,512]{1,0:T(8,128)(2,1)} %bitcast.39, bf16[2048,512]{1,0:T(8,128)(2,1)} %bitcast.38), custom_call_target="tpu_custom_call" | custom-call | tf_op jit(solution)/shard_map/pallas_call | solution.py:347
  113.5 1.9 %convolution_convert_fusion = bf16[16,96,512]{2,1,0:T(8,128)(2,1)S(1)} fusion(bf16[16,64,512]{2,1,0:T(8,128)(2,1)} %get-tuple-element.13, s32[16,96]{1,0:T(8,128)S(1)} %pad_add_fusion.1, s32[96]{0:T(128)S(1)} %get-tuple-element.26, s32[96]{0:T(128)S(1)} %get-tuple-element.27, pred[16,96]{1,0:T(8,128)(4,1)S(1)} %broadcast_compare_fusion, ...), kind=kOutput, calls=%fused_computation.9 | convolution fusion | flops 102137856 | bytes 2629984 | tf_op jit(solution)/shard_map/jrt,jrh->jth/dot_general | solution.py:436
  115.3 0.2 fusion.55
  115.5 1.4 %copy-done.2 = bf16[2,2,2,2,32,2048]{5,4,3,2,1,0:T(8,128)(2,1)S(1)} copy-done((bf16[2,2,2,2,32,2048]{5,4,3,2,1,0:T(8,128)(2,1)S(1)}, bf16[2,2,2,2,32,2048]{5,4,3,2,1,0:T(8,128)(2,1)}, u32[]{:S(2)}) %copy-start.2) | copy-done | bytes 2097176
  116.9 3.3 %convolution_bitcast_fusion = f32[1,2048,512]{2,1,0:T(8,128)} fusion(bf16[512,2048]{1,0:T(8,128)(2,1)S(1)} %bitcast.40, bf16[512,512]{1,0:T(8,128)(2,1)S(1)} %bitcast.46), kind=kOutput, calls=%fused_computation.4 | convolution fusion | flops 1073741824 | bytes 6815744 | tf_op jit(solution)/shard_map/dot_general | solution.py:447
  120.2 3.3 %convolution_bitcast_fusion.1 = f32[1,2048,512]{2,1,0:T(8,128)} fusion(bf16[512,2048]{1,0:T(8,128)(2,1)S(1)} %bitcast.49, bf16[512,512]{1,0:T(8,128)(2,1)S(1)} %bitcast.45), kind=kOutput, calls=%fused_computation.5 | convolution fusion | flops 1073741824 | bytes 6815744 | tf_op jit(solution)/shard_map/dot_general | solution.py:446
  123.5 3.3 %convolution_bitcast_fusion.2 = f32[1,2048,512]{2,1,0:T(8,128)} fusion(bf16[512,2048]{1,0:T(8,128)(2,1)S(1)} %bitcast.50, bf16[512,512]{1,0:T(8,128)(2,1)S(1)} %bitcast.44), kind=kOutput, calls=%fused_computation.6 | convolution fusion | flops 1073741824 | bytes 6815744 | tf_op jit(solution)/shard_map/dot_general | solution.py:445
  126.9 0.6 copy.17
  (25 shorter events, 0.4 us)
Async XLA Ops:
  0.6 50.0 %copy-start = (bf16[1,2048,512]{2,1,0:T(8,128)(2,1)S(1)}, bf16[1,2048,512]{2,1,0:T(8,128)(2,1)}, u32[]{:S(2)}) copy-start(bf16[1,2048,512]{2,1,0:T(8,128)(2,1)} %param.15) | copy-start | bytes 6291460
  44.9 3.6 %copy-start.3 = (bf16[2,2,2,2,32,2048]{5,4,3,2,1,0:T(8,128)(2,1)S(1)}, bf16[2,2,2,2,32,2048]{5,4,3,2,1,0:T(8,128)(2,1)}, u32[]{:S(2)}) copy-start(bf16[2,2,2,2,32,2048]{5,4,3,2,1,0:T(8,128)(2,1)} %get-tuple-element.10) | copy-start | bytes 6291460
  50.6 1.6 %copy-start.1 = (bf16[1,2048,512]{2,1,0:T(8,128)(2,1)S(1)}, bf16[1,2048,512]{2,1,0:T(8,128)(2,1)}, u32[]{:S(2)}) copy-start(bf16[1,2048,512]{2,1,0:T(8,128)(2,1)} %param.13) | copy-start | bytes 6291460
  50.6 2.2 %copy-start.7 = (bf16[2,2,2,2,32,2048]{5,4,3,2,1,0:T(8,128)(2,1)S(1)}, bf16[2,2,2,2,32,2048]{5,4,3,2,1,0:T(8,128)(2,1)}, u32[]{:S(2)}) copy-start(bf16[2,2,2,2,32,2048]{5,4,3,2,1,0:T(8,128)(2,1)} %get-tuple-element.11) | copy-start | bytes 6291460
  54.5 1.4 %copy-start.4 = (bf16[512,512]{1,0:T(8,128)(2,1)}, bf16[512,512]{1,0:T(8,128)(2,1)S(1)}, u32[]{:S(2)}) copy-start(bf16[512,512]{1,0:T(8,128)(2,1)S(1)} %get-tuple-element.18.g_back) | copy-start | bytes 1572868
  54.5 1.4 %copy-start.5 = (bf16[512,512]{1,0:T(8,128)(2,1)}, bf16[512,512]{1,0:T(8,128)(2,1)S(1)}, u32[]{:S(2)}) copy-start(bf16[512,512]{1,0:T(8,128)(2,1)S(1)} %get-tuple-element.19.u_back) | copy-start | bytes 1572868
  115.3 1.6 %copy-start.2 = (bf16[2,2,2,2,32,2048]{5,4,3,2,1,0:T(8,128)(2,1)S(1)}, bf16[2,2,2,2,32,2048]{5,4,3,2,1,0:T(8,128)(2,1)}, u32[]{:S(2)}) copy-start(bf16[2,2,2,2,32,2048]{5,4,3,2,1,0:T(8,128)(2,1)} %get-tuple-element.16) | copy-start | bytes 6291460
  116.9 3.3 %copy-start.8 = (bf16[2,2,2,2,32,2048]{5,4,3,2,1,0:T(8,128)(2,1)S(1)}, bf16[2,2,2,2,32,2048]{5,4,3,2,1,0:T(8,128)(2,1)}, u32[]{:S(2)}) copy-start(bf16[2,2,2,2,32,2048]{5,4,3,2,1,0:T(8,128)(2,1)} %get-tuple-element.11) | copy-start | bytes 6291460
  123.5 3.3 %copy-start.6 = (bf16[32,1024]{1,0:T(8,128)(2,1)S(1)}, bf16[32,1024]{1,0:T(8,128)(2,1)}, u32[]{:S(2)}) copy-start(bf16[32,1024]{1,0:T(8,128)(2,1)} %get-tuple-element.32) | copy-start | bytes 196612

commit v6 on v5

--- a/solution.py
+++ b/solution.py
@@ -121,7 +121,7 @@
         functools.partial(gather_kernel, n_expert, n_dp),
         out_shape=(wide, wide, small),
         in_specs=[pl.BlockSpec(memory_space=pltpu.VMEM)] * 3,
-        out_specs=[pl.BlockSpec(memory_space=pl.ANY)] * 3,
+        out_specs=[pl.BlockSpec(memory_space=pltpu.VMEM)] * 3,
         scratch_shapes=[
             pltpu.SemaphoreType.DMA((5, steps)),
             pltpu.SemaphoreType.DMA((5, steps)),

time: 128 us -> 127 us (level)
  no operation moved by 1% of the time
where the time goes in v6:
time: 127 us; the launch traced here: 126 us
  Pallas kernels  94.3 us (74%)
  matrix products  20 us (16%)
  other arithmetic  6.4 us (5%)
  local copies, waits for them, and re-layouts  4.78 us (4%)
    pallas_call x1, Pallas kernels, exchange(): pl.pallas_call(functools.partial(exchange_kernel, n_expert, n_dp, chunks)...  57.4 us
    pallas_call x1, Pallas kernels, gather_all(): pl.pallas_call(functools.partial(gather_kernel, n_expert, n_dp), out_shap...  36.9 us
    unnamed x21, local copies, waits for them, and re-layouts  4.57 us
    dot_general x1, matrix products, local(): upper = jnp.dot(rows, w_up, preferred_element_type=jnp.float32)  3.62 us
    dot_general x1, matrix products, local(): lax.dot_general(rows, take(0), contract_rows, preferred_element_type=jnp....  3.32 us
    dot_general x1, matrix products, local(): lax.dot_general(p_grads, take(2), contract_rows, preferred_element_type=j...  3.32 us
    dot_general x1, matrix products, local(): lax.dot_general(rows, take(1), contract_rows, preferred_element_type=jnp....  3.32 us

profile of v6, /device:TPU:0, one launch (start us, length us, event | category | flops | bytes accessed | tf_op | source)
XLA Modules:
  0.0 126.3 jit_solution(5764692180796911607)
XLA Ops:
  0.6 1.4 %fusion.39 = s32[]{:T(128)} fusion(s32[16]{0:T(128)} %match.1, s32[]{:T(128)S(6)} %axis_index.12), kind=kLoop, calls=%fused_computation.71 | loop fusion | flops 47 | bytes 72 | tf_op jit(solution)/shard_map/reduce_sum | solution.py:433
  2.1 0.6 iota_compare_fusion.4
  2.8 0.8 copy.14
  3.5 0.8 copy.15
  4.3 0.7 select_reduce_fusion.2.table
  5.1 36.9 %shard_map.111 = (bf16[2,2,2,2,32,2048]{5,4,3,2,1,0:T(8,128)(2,1)}, bf16[2,2,2,2,32,2048]{5,4,3,2,1,0:T(8,128)(2,1)}, f32[2,2,2,2,32,128]{5,4,3,2,1,0:T(8,128)}) custom-call(bf16[32,1024]{1,0:T(8,128)(2,1)} %tokens.1, bf16[32,1024]{1,0:T(8,128)(2,1)} %cotangent.1, f32[32,128]{1,0:T(8,128)} %select_reduce_fusion.2.table), custom_call_target="tpu_custom_call" | custom-call | tf_op jit(solution)/shard_map/pallas_call | solution.py:120
  42.0 1.2 select_reduce_fusion
  43.2 0.1 fusion.16
  43.5 0.1 fusion.14
  43.8 3.6 %fusion.43 = f32[512,512]{1,0:T(8,128)S(1)} fusion(bf16[512,2048]{1,0:T(8,128)(2,1)} %bitcast.47, bf16[1,2048,512]{2,1,0:T(8,128)(2,1)} %param.14), kind=kOutput, calls=%fused_computation.78 | convolution fusion | flops 1073741824 | bytes 5242880 | tf_op jit(solution)/shard_map/dot_general | solution.py:418
  47.4 2.0 %fusion.1 = (bf16[2,2,2,2,32,2048]{5,4,3,2,1,0:T(8,128)(2,1)}, bf16[2,2,2,2,32,2048]{5,4,3,2,1,0:T(8,128)(2,1)S(1)}) fusion(bf16[2,2,2,2,32,2048]{5,4,3,2,1,0:T(8,128)(2,1)S(1)} %copy-done.3, f32[2,2,2,2,32]{4,3,2,1,0:T(2,128)S(1)} %get-tuple-element.14, f32[2,2,2,2,32]{4,3,2,1,0:T(2,128)S(1)} %get-tuple-element.15), kind=kLoop, calls=%fused_computation.3 | loop fusion | flops 5242880 | bytes 6295552 | tf_op jit(solution)/shard_map/convert_element_type | solution.py:382
  49.5 1.2 fusion.2
  50.7 0.3 copy-done.1
  51.1 0.6 copy-done.7
  51.7 1.7 %multiply_convert_fusion.2 = (bf16[512,512]{1,0:T(8,128)(2,1)S(1)}, bf16[512,512]{1,0:T(8,128)(2,1)S(1)}, bf16[512,512]{1,0:T(8,128)(2,1)S(1)}) fusion(f32[512,512]{1,0:T(8,128)S(1)} %fusion.2, f32[512,512]{1,0:T(8,128)S(1)} %fusion.43, bf16[512,2048]{1,0:T(8,128)(2,1)S(1)} %bitcast.48, bf16[1,2048,512]{2,1,0:T(8,128)(2,1)S(1)} %copy-done.1), kind=kOutput, calls=%fused_computation.25 | convolution fusion | flops 1077936128 | bytes 7864320 | tf_op jit(solution)/shard_map/dot_general | solution.py:417
  53.4 1.4 %fusion.10.packed = bf16[16,64,512]{2,1,0:T(8,128)(2,1)} fusion(bf16[16,32,512]{2,1,0:T(8,128)(2,1)S(1)} %bitcast.51, bf16[16,32,512]{2,1,0:T(8,128)(2,1)S(1)} %bitcast.43, bf16[16,32,512]{2,1,0:T(8,128)(2,1)S(1)} %bitcast.42, s32[96]{0:T(128)S(1)} %get-tuple-element.26, s32[96]{0:T(128)S(1)} %get-tuple-element.27, s32[16,96]{1,0:T(8,128)S(1)} %pad_add_fusion, ...), kind=kOutput, calls=%fused_computation.16 | convolution fusion | flops 106594304 | bytes 2629984 | tf_op jit(solution)/shard_map/jrt,jth->jrh/dot_general | solution.py:427
  54.8 57.4 %shard_map.112 = (bf16[16,64,512]{2,1,0:T(8,128)(2,1)}, bf16[32,1024]{1,0:T(8,128)(2,1)}) custom-call(s32[16]{0:T(128)} %match.1, bf16[16,64,512]{2,1,0:T(8,128)(2,1)} %fusion.10.packed, bf16[512,512]{1,0:T(8,128)(2,1)} %copy-done.4, bf16[512,512]{1,0:T(8,128)(2,1)} %copy-done.5, bf16[2048,512]{1,0:T(8,128)(2,1)} %bitcast.39, bf16[2048,512]{1,0:T(8,128)(2,1)} %bitcast.38), custom_call_target="tpu_custom_call" | custom-call | tf_op jit(solution)/shard_map/pallas_call | solution.py:347
  112.3 1.9 %convolution_convert_fusion = bf16[16,96,512]{2,1,0:T(8,128)(2,1)S(1)} fusion(bf16[16,64,512]{2,1,0:T(8,128)(2,1)} %get-tuple-element.13, s32[16,96]{1,0:T(8,128)S(1)} %pad_add_fusion.1, s32[96]{0:T(128)S(1)} %get-tuple-element.26, s32[96]{0:T(128)S(1)} %get-tuple-element.27, pred[16,96]{1,0:T(8,128)(4,1)S(1)} %broadcast_compare_fusion, ...), kind=kOutput, calls=%fused_computation.9 | convolution fusion | flops 102137856 | bytes 2629984 | tf_op jit(solution)/shard_map/jrt,jrh->jth/dot_general | solution.py:436
  114.1 0.2 fusion.55
  114.3 1.4 %copy-done.2 = bf16[2,2,2,2,32,2048]{5,4,3,2,1,0:T(8,128)(2,1)S(1)} copy-done((bf16[2,2,2,2,32,2048]{5,4,3,2,1,0:T(8,128)(2,1)S(1)}, bf16[2,2,2,2,32,2048]{5,4,3,2,1,0:T(8,128)(2,1)}, u32[]{:S(2)}) %copy-start.2) | copy-done | bytes 2097176
  115.7 3.3 %convolution_bitcast_fusion = f32[1,2048,512]{2,1,0:T(8,128)} fusion(bf16[512,2048]{1,0:T(8,128)(2,1)S(1)} %bitcast.40, bf16[512,512]{1,0:T(8,128)(2,1)S(1)} %bitcast.46), kind=kOutput, calls=%fused_computation.4 | convolution fusion | flops 1073741824 | bytes 6815744 | tf_op jit(solution)/shard_map/dot_general | solution.py:447
  119.0 3.3 %convolution_bitcast_fusion.1 = f32[1,2048,512]{2,1,0:T(8,128)} fusion(bf16[512,2048]{1,0:T(8,128)(2,1)S(1)} %bitcast.49, bf16[512,512]{1,0:T(8,128)(2,1)S(1)} %bitcast.45), kind=kOutput, calls=%fused_computation.5 | convolution fusion | flops 1073741824 | bytes 6815744 | tf_op jit(solution)/shard_map/dot_general | solution.py:446
  122.4 3.3 %convolution_bitcast_fusion.2 = f32[1,2048,512]{2,1,0:T(8,128)} fusion(bf16[512,2048]{1,0:T(8,128)(2,1)S(1)} %bitcast.50, bf16[512,512]{1,0:T(8,128)(2,1)S(1)} %bitcast.44), kind=kOutput, calls=%fused_computation.6 | convolution fusion | flops 1073741824 | bytes 6815744 | tf_op jit(solution)/shard_map/dot_general | solution.py:445
  125.7 0.6 copy.17
  (25 shorter events, 0.4 us)
Async XLA Ops:
  0.6 48.8 %copy-start = (bf16[1,2048,512]{2,1,0:T(8,128)(2,1)S(1)}, bf16[1,2048,512]{2,1,0:T(8,128)(2,1)}, u32[]{:S(2)}) copy-start(bf16[1,2048,512]{2,1,0:T(8,128)(2,1)} %param.15) | copy-start | bytes 6291460
  43.8 3.6 %copy-start.3 = (bf16[2,2,2,2,32,2048]{5,4,3,2,1,0:T(8,128)(2,1)S(1)}, bf16[2,2,2,2,32,2048]{5,4,3,2,1,0:T(8,128)(2,1)}, u32[]{:S(2)}) copy-start(bf16[2,2,2,2,32,2048]{5,4,3,2,1,0:T(8,128)(2,1)} %get-tuple-element.10) | copy-start | bytes 6291460
  49.5 1.6 %copy-start.1 = (bf16[1,2048,512]{2,1,0:T(8,128)(2,1)S(1)}, bf16[1,2048,512]{2,1,0:T(8,128)(2,1)}, u32[]{:S(2)}) copy-start(bf16[1,2048,512]{2,1,0:T(8,128)(2,1)} %param.13) | copy-start | bytes 6291460
  49.5 2.2 %copy-start.7 = (bf16[2,2,2,2,32,2048]{5,4,3,2,1,0:T(8,128)(2,1)S(1)}, bf16[2,2,2,2,32,2048]{5,4,3,2,1,0:T(8,128)(2,1)}, u32[]{:S(2)}) copy-start(bf16[2,2,2,2,32,2048]{5,4,3,2,1,0:T(8,128)(2,1)} %get-tuple-element.11) | copy-start | bytes 6291460
  53.4 1.4 %copy-start.4 = (bf16[512,512]{1,0:T(8,128)(2,1)}, bf16[512,512]{1,0:T(8,128)(2,1)S(1)}, u32[]{:S(2)}) copy-start(bf16[512,512]{1,0:T(8,128)(2,1)S(1)} %get-tuple-element.18.g_back) | copy-start | bytes 1572868
  53.4 1.4 %copy-start.5 = (bf16[512,512]{1,0:T(8,128)(2,1)}, bf16[512,512]{1,0:T(8,128)(2,1)S(1)}, u32[]{:S(2)}) copy-start(bf16[512,512]{1,0:T(8,128)(2,1)S(1)} %get-tuple-element.19.u_back) | copy-start | bytes 1572868
  114.1 1.6 %copy-start.2 = (bf16[2,2,2,2,32,2048]{5,4,3,2,1,0:T(8,128)(2,1)S(1)}, bf16[2,2,2,2,32,2048]{5,4,3,2,1,0:T(8,128)(2,1)}, u32[]{:S(2)}) copy-start(bf16[2,2,2,2,32,2048]{5,4,3,2,1,0:T(8,128)(2,1)} %get-tuple-element.16) | copy-start | bytes 6291460
  115.7 3.3 %copy-start.8 = (bf16[2,2,2,2,32,2048]{5,4,3,2,1,0:T(8,128)(2,1)S(1)}, bf16[2,2,2,2,32,2048]{5,4,3,2,1,0:T(8,128)(2,1)}, u32[]{:S(2)}) copy-start(bf16[2,2,2,2,32,2048]{5,4,3,2,1,0:T(8,128)(2,1)} %get-tuple-element.11) | copy-start | bytes 6291460
  122.4 3.3 %copy-start.6 = (bf16[32,1024]{1,0:T(8,128)(2,1)S(1)}, bf16[32,1024]{1,0:T(8,128)(2,1)}, u32[]{:S(2)}) copy-start(bf16[32,1024]{1,0:T(8,128)(2,1)} %get-tuple-element.32) | copy-start | bytes 196612

commit v7 on v6

--- a/solution.py
+++ b/solution.py
@@ -288,7 +288,7 @@
     for i in range(halves):
         start_step(i, 0)
 
-    early = min(2, steps - 1)
+    early = steps - 2
     for s in range(early):
         for i in range(halves):
             end_step(i, s)
@@ -308,16 +308,17 @@
         pltpu.make_async_copy(
             ordered.at[0, rows_of(c)], landed.at[e, rows_of(c)], own.at[1, c]
         ).start()
+        if c == chunks - 1:
+            for i in range(halves):
+                end_step(i, early)
+                start_step(i, early + 1)
 
         @pl.loop(1, n_expert)
         def _(o):
             second(c, o).start()
 
-    for s in range(early, steps):
-        for i in range(halves):
-            end_step(i, s)
-            if s + 1 < steps:
-                start_step(i, s + 1)
+    for i in range(halves):
+        end_step(i, steps - 1)
     for i in range(halves):
         result[pl.ds(i * half, half), :] = sums[i][steps - 1][...]
     for c in range(chunks):

time: 127 us -> 124 us (0.976)
  Pallas kernels: 94.3 us -> 90.7 us
    pallas_call x1, Pallas kernels: 57.4 us -> 53.8 us  [exchange(): pl.pallas_call(functools.partial(exchange_kernel, n_expert, n_dp, chunks)...]
where the time goes in v7:
time: 124 us; the launch traced here: 123 us
  Pallas kernels  90.7 us (73%)
  matrix products  20 us (16%)
  other arithmetic  6.4 us (5%)
  local copies, waits for them, and re-layouts  4.78 us (4%)
    pallas_call x1, Pallas kernels, exchange(): pl.pallas_call(functools.partial(exchange_kernel, n_expert, n_dp, chunks)...  53.8 us
    pallas_call x1, Pallas kernels, gather_all(): pl.pallas_call(functools.partial(gather_kernel, n_expert, n_dp), out_shap...  36.9 us
    unnamed x21, local copies, waits for them, and re-layouts  4.57 us
    dot_general x1, matrix products, local(): upper = jnp.dot(rows, w_up, preferred_element_type=jnp.float32)  3.62 us
    dot_general x1, matrix products, local(): lax.dot_general(rows, take(0), contract_rows, preferred_element_type=jnp....  3.32 us
    dot_general x1, matrix products, local(): lax.dot_general(rows, take(1), contract_rows, preferred_element_type=jnp....  3.32 us
    dot_general x1, matrix products, local(): lax.dot_general(p_grads, take(2), contract_rows, preferred_element_type=j...  3.32 us

profile of v7, /device:TPU:0, one launch (start us, length us, event | category | flops | bytes accessed | tf_op | source)
XLA Modules:
  0.0 122.7 jit_solution(10914512579275467808)
XLA Ops:
  0.6 1.4 %fusion.39 = s32[]{:T(128)} fusion(s32[16]{0:T(128)} %match.1, s32[]{:T(128)S(6)} %axis_index.12), kind=kLoop, calls=%fused_computation.71 | loop fusion | flops 47 | bytes 72 | tf_op jit(solution)/shard_map/reduce_sum | solution.py:434
  2.1 0.6 iota_compare_fusion.4
  2.8 0.8 copy.14
  3.5 0.8 copy.15
  4.3 0.7 select_reduce_fusion.2.table
  5.1 36.9 %shard_map.111 = (bf16[2,2,2,2,32,2048]{5,4,3,2,1,0:T(8,128)(2,1)}, bf16[2,2,2,2,32,2048]{5,4,3,2,1,0:T(8,128)(2,1)}, f32[2,2,2,2,32,128]{5,4,3,2,1,0:T(8,128)}) custom-call(bf16[32,1024]{1,0:T(8,128)(2,1)} %tokens.1, bf16[32,1024]{1,0:T(8,128)(2,1)} %cotangent.1, f32[32,128]{1,0:T(8,128)} %select_reduce_fusion.2.table), custom_call_target="tpu_custom_call" | custom-call | tf_op jit(solution)/shard_map/pallas_call | solution.py:120
  42.0 1.2 select_reduce_fusion
  43.2 0.1 fusion.16
  43.5 0.1 fusion.14
  43.8 3.6 %fusion.43 = f32[512,512]{1,0:T(8,128)S(1)} fusion(bf16[512,2048]{1,0:T(8,128)(2,1)} %bitcast.47, bf16[1,2048,512]{2,1,0:T(8,128)(2,1)} %param.14), kind=kOutput, calls=%fused_computation.78 | convolution fusion | flops 1073741824 | bytes 5242880 | tf_op jit(solution)/shard_map/dot_general | solution.py:419
  47.4 2.0 %fusion.1 = (bf16[2,2,2,2,32,2048]{5,4,3,2,1,0:T(8,128)(2,1)}, bf16[2,2,2,2,32,2048]{5,4,3,2,1,0:T(8,128)(2,1)S(1)}) fusion(bf16[2,2,2,2,32,2048]{5,4,3,2,1,0:T(8,128)(2,1)S(1)} %copy-done.3, f32[2,2,2,2,32]{4,3,2,1,0:T(2,128)S(1)} %get-tuple-element.14, f32[2,2,2,2,32]{4,3,2,1,0:T(2,128)S(1)} %get-tuple-element.15), kind=kLoop, calls=%fused_computation.3 | loop fusion | flops 5242880 | bytes 6295552 | tf_op jit(solution)/shard_map/convert_element_type | solution.py:383
  49.5 1.2 %fusion.2 = f32[512,512]{1,0:T(8,128)S(1)} fusion(bf16[512,2048]{1,0:T(8,128)(2,1)S(1)} %bitcast.41, bf16[1,2048,512]{2,1,0:T(8,128)(2,1)S(1)} %copy-done), kind=kOutput, calls=%fused_computation.7 | convolution fusion | flops 1073741824 | bytes 5242880 | tf_op jit(solution)/shard_map/dot_general | solution.py:422
  50.7 0.3 copy-done.1
  51.1 0.6 copy-done.7
  51.7 1.7 %multiply_convert_fusion.2 = (bf16[512,512]{1,0:T(8,128)(2,1)S(1)}, bf16[512,512]{1,0:T(8,128)(2,1)S(1)}, bf16[512,512]{1,0:T(8,128)(2,1)S(1)}) fusion(f32[512,512]{1,0:T(8,128)S(1)} %fusion.2, f32[512,512]{1,0:T(8,128)S(1)} %fusion.43, bf16[512,2048]{1,0:T(8,128)(2,1)S(1)} %bitcast.48, bf16[1,2048,512]{2,1,0:T(8,128)(2,1)S(1)} %copy-done.1), kind=kOutput, calls=%fused_computation.25 | convolution fusion | flops 1077936128 | bytes 7864320 | tf_op jit(solution)/shard_map/dot_general | solution.py:418
  53.4 1.4 %fusion.10.packed = bf16[16,64,512]{2,1,0:T(8,128)(2,1)} fusion(bf16[16,32,512]{2,1,0:T(8,128)(2,1)S(1)} %bitcast.51, bf16[16,32,512]{2,1,0:T(8,128)(2,1)S(1)} %bitcast.43, bf16[16,32,512]{2,1,0:T(8,128)(2,1)S(1)} %bitcast.42, s32[96]{0:T(128)S(1)} %get-tuple-element.26, s32[96]{0:T(128)S(1)} %get-tuple-element.27, s32[16,96]{1,0:T(8,128)S(1)} %pad_add_fusion, ...), kind=kOutput, calls=%fused_computation.16 | convolution fusion | flops 106594304 | bytes 2629984 | tf_op jit(solution)/shard_map/jrt,jth->jrh/dot_general | solution.py:428
  54.8 53.8 %shard_map.112 = (bf16[16,64,512]{2,1,0:T(8,128)(2,1)}, bf16[32,1024]{1,0:T(8,128)(2,1)}) custom-call(s32[16]{0:T(128)} %match.1, bf16[16,64,512]{2,1,0:T(8,128)(2,1)} %fusion.10.packed, bf16[512,512]{1,0:T(8,128)(2,1)} %copy-done.4, bf16[512,512]{1,0:T(8,128)(2,1)} %copy-done.5, bf16[2048,512]{1,0:T(8,128)(2,1)} %bitcast.39, bf16[2048,512]{1,0:T(8,128)(2,1)} %bitcast.38), custom_call_target="tpu_custom_call" | custom-call | tf_op jit(solution)/shard_map/pallas_call | solution.py:348
  108.6 1.9 %convolution_convert_fusion = bf16[16,96,512]{2,1,0:T(8,128)(2,1)S(1)} fusion(bf16[16,64,512]{2,1,0:T(8,128)(2,1)} %get-tuple-element.13, s32[16,96]{1,0:T(8,128)S(1)} %pad_add_fusion.1, s32[96]{0:T(128)S(1)} %get-tuple-element.26, s32[96]{0:T(128)S(1)} %get-tuple-element.27, pred[16,96]{1,0:T(8,128)(4,1)S(1)} %broadcast_compare_fusion, ...), kind=kOutput, calls=%fused_computation.9 | convolution fusion | flops 102137856 | bytes 2629984 | tf_op jit(solution)/shard_map/jrt,jrh->jth/dot_general | solution.py:437
  110.5 0.2 fusion.55
  110.7 1.4 %copy-done.2 = bf16[2,2,2,2,32,2048]{5,4,3,2,1,0:T(8,128)(2,1)S(1)} copy-done((bf16[2,2,2,2,32,2048]{5,4,3,2,1,0:T(8,128)(2,1)S(1)}, bf16[2,2,2,2,32,2048]{5,4,3,2,1,0:T(8,128)(2,1)}, u32[]{:S(2)}) %copy-start.2) | copy-done | bytes 2097176
  112.1 3.3 %convolution_bitcast_fusion = f32[1,2048,512]{2,1,0:T(8,128)} fusion(bf16[512,2048]{1,0:T(8,128)(2,1)S(1)} %bitcast.40, bf16[512,512]{1,0:T(8,128)(2,1)S(1)} %bitcast.46), kind=kOutput, calls=%fused_computation.4 | convolution fusion | flops 1073741824 | bytes 6815744 | tf_op jit(solution)/shard_map/dot_general | solution.py:448
  115.4 3.3 %convolution_bitcast_fusion.1 = f32[1,2048,512]{2,1,0:T(8,128)} fusion(bf16[512,2048]{1,0:T(8,128)(2,1)S(1)} %bitcast.49, bf16[512,512]{1,0:T(8,128)(2,1)S(1)} %bitcast.45), kind=kOutput, calls=%fused_computation.5 | convolution fusion | flops 1073741824 | bytes 6815744 | tf_op jit(solution)/shard_map/dot_general | solution.py:447
  118.7 3.3 %convolution_bitcast_fusion.2 = f32[1,2048,512]{2,1,0:T(8,128)} fusion(bf16[512,2048]{1,0:T(8,128)(2,1)S(1)} %bitcast.50, bf16[512,512]{1,0:T(8,128)(2,1)S(1)} %bitcast.44), kind=kOutput, calls=%fused_computation.6 | convolution fusion | flops 1073741824 | bytes 6815744 | tf_op jit(solution)/shard_map/dot_general | solution.py:446
  122.0 0.6 copy.17
  (25 shorter events, 0.4 us)
Async XLA Ops:
  0.6 48.8 %copy-start = (bf16[1,2048,512]{2,1,0:T(8,128)(2,1)S(1)}, bf16[1,2048,512]{2,1,0:T(8,128)(2,1)}, u32[]{:S(2)}) copy-start(bf16[1,2048,512]{2,1,0:T(8,128)(2,1)} %param.15) | copy-start | bytes 6291460
  43.8 3.6 %copy-start.3 = (bf16[2,2,2,2,32,2048]{5,4,3,2,1,0:T(8,128)(2,1)S(1)}, bf16[2,2,2,2,32,2048]{5,4,3,2,1,0:T(8,128)(2,1)}, u32[]{:S(2)}) copy-start(bf16[2,2,2,2,32,2048]{5,4,3,2,1,0:T(8,128)(2,1)} %get-tuple-element.10) | copy-start | bytes 6291460
  49.5 1.6 %copy-start.1 = (bf16[1,2048,512]{2,1,0:T(8,128)(2,1)S(1)}, bf16[1,2048,512]{2,1,0:T(8,128)(2,1)}, u32[]{:S(2)}) copy-start(bf16[1,2048,512]{2,1,0:T(8,128)(2,1)} %param.13) | copy-start | bytes 6291460
  49.5 2.2 %copy-start.7 = (bf16[2,2,2,2,32,2048]{5,4,3,2,1,0:T(8,128)(2,1)S(1)}, bf16[2,2,2,2,32,2048]{5,4,3,2,1,0:T(8,128)(2,1)}, u32[]{:S(2)}) copy-start(bf16[2,2,2,2,32,2048]{5,4,3,2,1,0:T(8,128)(2,1)} %get-tuple-element.11) | copy-start | bytes 6291460
  53.4 1.4 %copy-start.4 = (bf16[512,512]{1,0:T(8,128)(2,1)}, bf16[512,512]{1,0:T(8,128)(2,1)S(1)}, u32[]{:S(2)}) copy-start(bf16[512,512]{1,0:T(8,128)(2,1)S(1)} %get-tuple-element.18.g_back) | copy-start | bytes 1572868
  53.4 1.4 %copy-start.5 = (bf16[512,512]{1,0:T(8,128)(2,1)}, bf16[512,512]{1,0:T(8,128)(2,1)S(1)}, u32[]{:S(2)}) copy-start(bf16[512,512]{1,0:T(8,128)(2,1)S(1)} %get-tuple-element.19.u_back) | copy-start | bytes 1572868
  110.5 1.6 %copy-start.2 = (bf16[2,2,2,2,32,2048]{5,4,3,2,1,0:T(8,128)(2,1)S(1)}, bf16[2,2,2,2,32,2048]{5,4,3,2,1,0:T(8,128)(2,1)}, u32[]{:S(2)}) copy-start(bf16[2,2,2,2,32,2048]{5,4,3,2,1,0:T(8,128)(2,1)} %get-tuple-element.16) | copy-start | bytes 6291460
  112.1 3.3 %copy-start.8 = (bf16[2,2,2,2,32,2048]{5,4,3,2,1,0:T(8,128)(2,1)S(1)}, bf16[2,2,2,2,32,2048]{5,4,3,2,1,0:T(8,128)(2,1)}, u32[]{:S(2)}) copy-start(bf16[2,2,2,2,32,2048]{5,4,3,2,1,0:T(8,128)(2,1)} %get-tuple-element.11) | copy-start | bytes 6291460
  118.7 3.3 %copy-start.6 = (bf16[32,1024]{1,0:T(8,128)(2,1)S(1)}, bf16[32,1024]{1,0:T(8,128)(2,1)}, u32[]{:S(2)}) copy-start(bf16[32,1024]{1,0:T(8,128)(2,1)} %get-tuple-element.32) | copy-start | bytes 196612
